TPU v7x, 32 devices: a whole 2x2x4 slice. The times are simulated.
32 devices in a mesh: gx: 8 (over z, x), yz: 4 (over y, core).
Axes of the slice: x: 2, y: 2, z: 4, core: 2. Of those that a mesh axis runs over, the one named last changes fastest.
Arguments:
- residuals: float32 [32, 3, 64, 32, 128], P(None, None, 'gx', 'yz'), may hold values from -6 to 6
- vectors: float32 [8, 3, 64, 32, 128], P(None, None, 'gx', 'yz'), may hold values from -0.05 to 1.6
- phases: int32 [64, 32, 128], P('gx', 'yz'), may hold values from 0 to 7
- stiffness: float32 [8], replicated, may hold values from 0.5 to 4
Outputs:
- coarse_coeffs: float32 [256, 32], P(('gx', 'yz'))
- preconditioned: float32 [32, 3, 64, 32, 128], P(None, None, 'gx', 'yz')
All inputs are finite; a program needn't handle non-finite values.
Results may differ from a plain program's by a relative error of at most 0.0003.
Values sent between devices are 32-bit elements; how exact they have to be, the bound alone decides.
A program may use at most 192 MiB of HBM per device.

v0:
```python
import functools

import jax
import jax.numpy as jnp
from jax import lax
from jax.experimental import pallas as pl
from jax.experimental.pallas import tpu as pltpu
from jax.sharding import PartitionSpec as P

SWEEPS = 4


HIGH = lax.Precision.HIGHEST


def extended(cells, sides, width):
    for axis, dim in sides:
        count = lax.axis_size(axis)
        ends = count - 1
        head = lax.slice_in_dim(cells, 0, width, axis=dim)
        tail = lax.slice_in_dim(cells, cells.shape[dim] - width, cells.shape[dim], axis=dim)
        cells = jnp.concatenate(
            [
                lax.ppermute(tail, axis, [(i, (i + 1) % count) for i in range(ends)]),
                cells,
                lax.ppermute(head, axis, [((i + 1) % count, i) for i in range(ends)]),
            ],
            axis=dim,
        )
    return cells


def face_weights(modulus_ext):
    centre = modulus_ext[1:-1, 1:-1, :]
    zpadded = jnp.pad(centre, ((0, 0), (0, 0), (1, 1)))
    west_side = 0.5 * (centre + modulus_ext[:-2, 1:-1, :])
    east_side = 0.5 * (centre + modulus_ext[2:, 1:-1, :])
    south_side = 0.5 * (centre + modulus_ext[1:-1, :-2, :])
    north_side = 0.5 * (centre + modulus_ext[1:-1, 2:, :])
    lower_side = 0.5 * (centre + zpadded[:, :, :-2])
    upper_side = 0.5 * (centre + zpadded[:, :, 2:])
    diagonal_sum = 0.002 + west_side + east_side + south_side + north_side + lower_side + upper_side
    return (diagonal_sum, west_side, east_side, south_side, north_side, lower_side, upper_side)


def operate(values, weights):
    diagonal_sum, west_side, east_side, south_side, north_side, lower_side, upper_side = weights
    centre = values[..., 1:-1, 1:-1, :]
    spacing = [(0, 0)] * (values.ndim - 1) + [(1, 1)]
    zpadded = jnp.pad(centre, spacing)
    beside = west_side * values[..., :-2, 1:-1, :] + east_side * values[..., 2:, 1:-1, :]
    beside = beside + south_side * values[..., 1:-1, :-2, :] + north_side * values[..., 1:-1, 2:, :]
    beside = beside + lower_side * zpadded[..., :-2] + upper_side * zpadded[..., 2:]
    return diagonal_sum * centre - beside


def coarse_blocks(vectors_ext, modulus_ext):
    weights = face_weights(modulus_ext[1:-1, 1:-1, :])
    own_cells = vectors_ext[:, :, 2:-2, 2:-2, :]
    isolated = jnp.pad(own_cells, ((0, 0), (0, 0), (1, 1), (1, 1), (0, 0)))
    applied = operate(isolated, weights)
    self_block = jnp.einsum("kcxyz,lcxyz->kl", own_cells, applied, precision=HIGH)
    west_block = -jnp.einsum(
        "kcyz,lcyz->kl",
        weights[1][0] * own_cells[:, :, 0],
        vectors_ext[:, :, 1, 2:-2, :],
        precision=HIGH,
    )
    east_block = -jnp.einsum(
        "kcyz,lcyz->kl",
        weights[2][-1] * own_cells[:, :, -1],
        vectors_ext[:, :, -2, 2:-2, :],
        precision=HIGH,
    )
    south_block = -jnp.einsum(
        "kcxz,lcxz->kl",
        weights[3][:, 0] * own_cells[:, :, :, 0],
        vectors_ext[:, :, 2:-2, 1, :],
        precision=HIGH,
    )
    north_block = -jnp.einsum(
        "kcxz,lcxz->kl",
        weights[4][:, -1] * own_cells[:, :, :, -1],
        vectors_ext[:, :, 2:-2, -2, :],
        precision=HIGH,
    )
    return jnp.stack([self_block, west_block, east_block, south_block, north_block])


MESH = pl.DeviceIdType.MESH


def eliminate(rows, size):
    sublane = lax.broadcasted_iota(jnp.int32, rows[0].shape, 0)
    for p in range(size):
        reduced = []
        for a in rows:
            column = jnp.broadcast_to(a[:, p : p + 1], a.shape)
            pivot = a[p : p + 1, :] / column[p : p + 1, :]
            reduced.append(jnp.where(sublane == p, pivot, a - column * pivot))
        rows = reduced
    return rows


def product(a, b):
    return jnp.dot(a, b, precision=HIGH, preferred_element_type=jnp.float32)


def cyclic_solve(rows, size):
    count = len(rows)
    width = rows[0].shape[1]
    lane = lax.broadcasted_iota(jnp.int32, rows[0].shape, 1)
    is_own = lane < size
    is_low = (lane >= size) & (lane < 2 * size)
    is_high = (lane >= 2 * size) & (lane < 3 * size)
    is_rhs = lane >= 3 * size
    live = list(range(count))
    system = dict(enumerate(rows))
    levels = []
    while len(live) > 1:
        out = live[1::2]
        kept = live[0::2]
        solved = dict(zip(out, eliminate([system[i] for i in out], size)))
        fresh = {}
        for place, i in enumerate(kept):
            a = system[i]
            total = jnp.where(is_own | is_rhs, a, 0.0)
            if place > 0:
                t = product(a[:, size : 2 * size], solved[out[place - 1]])
                shifted = pltpu.roll(t, width - 2 * size, 1)
                total = total - jnp.where(is_own, shifted, jnp.where(is_low | is_rhs, t, 0.0))
            if place < len(out):
                t = product(a[:, 2 * size : 3 * size], solved[out[place]])
                shifted = pltpu.roll(t, width - size, 1)
                total = total - jnp.where(is_own, shifted, jnp.where(is_high | is_rhs, t, 0.0))
            fresh[i] = total
        levels.append((live, out, solved))
        system = fresh
        live = kept
    last = eliminate([system[live[0]]], size)[0]
    answer = {live[0]: last[:, 3 * size :]}
    for before, out, solved in reversed(levels):
        for i in out:
            a = solved[i]
            place = before.index(i)
            x = a[:, 3 * size :] - product(a[:, size : 2 * size], answer[before[place - 1]])
            if place + 1 < len(before):
                x = x - product(a[:, 2 * size : 3 * size], answer[before[place + 1]])
            answer[i] = x
    return [answer[i] for i in range(count)]


def coarse_kernel(
    count_x, count_y, width, panel, res, south_face, north_face,
    coeffs, grid, halo_x, halo_y, gathered, send_sem, recv_sem, halo_send, halo_recv
):
    index_x = lax.axis_index("gx")
    index_y = lax.axis_index("yz")
    count = count_x * count_y
    me = index_x * count_y + index_y
    barrier = pltpu.get_barrier_semaphore()

    def greet(step, carry):
        other = lax.rem(me + step, count)
        pl.semaphore_signal(
            barrier, inc=1, device_id=(other // count_y, lax.rem(other, count_y)), device_id_type=MESH
        )
        return carry

    lax.fori_loop(1, count, greet, 0)
    pl.semaphore_wait(barrier, count - 1)

    def sending(other, slot):
        return pltpu.make_async_remote_copy(
            src_ref=panel,
            dst_ref=gathered.at[slot],
            send_sem=send_sem.at[other],
            recv_sem=recv_sem.at[slot],
            device_id=(other // count_y, lax.rem(other, count_y)),
            device_id_type=MESH,
        )

    def send(step, carry):
        sending(lax.rem(me + step, count), me).start()
        return carry

    lax.fori_loop(1, count, send, 0)
    depth = res.shape[2]
    faces = (
        (index_x > 0, index_x < count_x - 1, res.at[:, :, 0], halo_x.at[1], (index_x - 1, index_y)),
        (index_x < count_x - 1, index_x > 0, res.at[:, :, depth - 1], halo_x.at[0], (index_x + 1, index_y)),
        (index_y > 0, index_y < count_y - 1, south_face, halo_y.at[1], (index_x, index_y - 1)),
        (index_y < count_y - 1, index_y > 0, north_face, halo_y.at[0], (index_x, index_y + 1)),
    )
    copies = []
    for slot, (sends, receives, source, target, device) in enumerate(faces):
        copy = pltpu.make_async_remote_copy(
            src_ref=source,
            dst_ref=target,
            send_sem=halo_send.at[slot],
            recv_sem=halo_recv.at[slot],
            device_id=device,
            device_id_type=MESH,
        )
        pl.when(sends)(copy.start)
        copies.append((sends, receives, copy))
    gathered[me] = panel[...]

    def collect(step, carry):
        other = lax.rem(me + step, count)
        sending(other, other).wait_recv()
        return carry

    lax.fori_loop(1, count, collect, 0)
    size = count_y * width
    rows = [
        gathered[pl.ds(g * count_y, count_y)].reshape(size, panel.shape[1]) for g in range(count_x)
    ]
    for g, x in enumerate(cyclic_solve(rows, size)):
        coeffs[pl.ds(g * size, size), :] = x
    slot = 0
    for step_x in (-1, 0, 1):
        for step_y in (-1, 0, 1):
            near_x = jnp.clip(index_x + step_x, 0, count_x - 1)
            near_y = jnp.clip(index_y + step_y, 0, count_y - 1)
            start = pl.multiple_of((near_x * count_y + near_y) * width, width)
            grid[pl.ds(slot * width, width), :] = coeffs[pl.ds(start, width), :]
            slot += 1

    def drain(step, carry):
        sending(lax.rem(me + step, count), me).wait_send()
        return carry

    lax.fori_loop(1, count, drain, 0)
    for sends, receives, copy in copies:
        pl.when(sends)(copy.wait_send)
        pl.when(receives)(copy.wait_recv)


def coarse_solve(panel, residuals, count_x, count_y, width):
    rhs, parts, depth, breadth, length = residuals.shape
    count = count_x * count_y
    vmem = pl.BlockSpec(memory_space=pltpu.VMEM)
    hbm = pl.BlockSpec(memory_space=pl.ANY)
    return pl.pallas_call(
        functools.partial(coarse_kernel, count_x, count_y, width),
        out_shape=(
            jax.ShapeDtypeStruct((count * width, rhs), jnp.float32),
            jax.ShapeDtypeStruct((9 * width, rhs), jnp.float32),
            jax.ShapeDtypeStruct((2, rhs, parts, breadth, length), jnp.float32),
            jax.ShapeDtypeStruct((2, rhs, parts, depth, length), jnp.float32),
        ),
        in_specs=[vmem, hbm, hbm, hbm],
        out_specs=(vmem, vmem, hbm, hbm),
        scratch_shapes=[
            pltpu.VMEM((count,) + panel.shape, jnp.float32),
            pltpu.SemaphoreType.DMA((count,)),
            pltpu.SemaphoreType.DMA((count,)),
            pltpu.SemaphoreType.DMA((4,)),
            pltpu.SemaphoreType.DMA((4,)),
        ],
        compiler_params=pltpu.CompilerParams(collective_id=0, has_side_effects=True),
    )(panel, residuals, residuals[:, :, :, 0, :], residuals[:, :, :, -1, :])


def panel_row(blocks, coarse_rhs, count_y):
    width = blocks.shape[1]
    columns = jnp.arange(count_y, dtype=jnp.int32)
    index_y = lax.axis_index("yz")

    def placed(block, offset):
        select = (columns == index_y + offset).astype(jnp.float32)
        return (block[:, None, :] * select[None, :, None]).reshape(width, count_y * width)

    own = placed(blocks[0], 0) + placed(blocks[3], -1) + placed(blocks[4], 1)
    return jnp.concatenate([own, placed(blocks[1], 0), placed(blocks[2], 0), coarse_rhs], axis=1)


def schwarz_kernel(
    rhs, parts, depth, breadth, width, res, vec, weights, cgrid, halo_x, halo_y, out,
    coeff, corr, forced, first, second
):
    length = res.shape[1]
    wide = breadth + 4
    own = depth * breadth

    for cls in range(9):
        for k in range(width):
            coeff[cls * width + k] = jnp.broadcast_to(
                cgrid[:, cls * width + k : cls * width + k + 1], (rhs, length)
            )
    zero = jnp.zeros((rhs, length), jnp.float32)
    for buffer in (first, second):
        def clear(i, carry, buffer=buffer):
            buffer[i] = zero
            return carry

        lax.fori_loop(0, (depth + 4) * wide, clear, 0)

    def component(part, carry):
        def region(cls, x0, nx, y0, ny):
            def one(i, carry):
                cell = (x0 + i // ny) * wide + y0 + lax.rem(i, ny)
                value = coeff[cls * width] * vec[part, cell, pl.ds(0, 1), :]
                for k in range(1, width):
                    value = value + coeff[cls * width + k] * vec[part, cell, pl.ds(k, 1), :]
                corr[cell] = value
                return carry

            lax.fori_loop(0, nx * ny, one, 0, unroll=2 if nx * ny > 1 else 1)

        spans_x = ((0, 2), (2, depth), (depth + 2, 2))
        spans_y = ((0, 2), (2, breadth), (breadth + 2, 2))
        for a, (x0, nx) in enumerate(spans_x):
            for b, (y0, ny) in enumerate(spans_y):
                if a != 1 and b != 1:
                    region(a * 3 + b, 1 if a == 0 else x0, 1, 1 if b == 0 else y0, 1)
                else:
                    region(a * 3 + b, x0, nx, y0, ny)

        def beside(buffer, x, y):
            cell = x * wide + y
            w = (x - 1) * (breadth + 2) + y - 1
            centre = buffer[cell]
            total = weights[w, pl.ds(1, 1), :] * buffer[cell - wide]
            total = total + weights[w, pl.ds(2, 1), :] * buffer[cell + wide]
            total = total + weights[w, pl.ds(3, 1), :] * buffer[cell - 1]
            total = total + weights[w, pl.ds(4, 1), :] * buffer[cell + 1]
            total = total + weights[w, pl.ds(5, 1), :] * pltpu.roll(centre, 1, 1)
            total = total + weights[w, pl.ds(6, 1), :] * pltpu.roll(centre, length - 1, 1)
            return centre, total

        def force(x, y, loaded, outer):
            cell = x * wide + y
            w = (x - 1) * (breadth + 2) + y - 1
            centre, total = beside(corr, x, y)
            scale = weights[w, pl.ds(0, 1), :]
            term = scale * loaded
            if outer:
                term = jnp.where(jnp.broadcast_to(scale, term.shape) > 0, term, 0.0)
            value = term - 0.8 * centre + total
            forced[cell] = value
            first[cell] = value

        def force_row(i, carry):
            for y in range(breadth):
                start = part * own + i * breadth + y
                force(i + 2, y + 2, res[pl.ds(start, rhs, stride=parts * own), :], False)
            for side in range(2):
                start = side * rhs * parts * depth + part * depth + i
                loaded = halo_y[pl.ds(start, rhs, stride=parts * depth), :]
                force(i + 2, 1 + side * (breadth + 1), loaded, True)
            return carry

        lax.fori_loop(0, depth, force_row, 0)

        def force_edge(i, carry):
            for side in range(2):
                start = side * rhs * parts * breadth + part * breadth + i
                loaded = halo_x[pl.ds(start, rhs, stride=parts * breadth), :]
                force(1 + side * (depth + 1), i + 2, loaded, True)
            return carry

        lax.fori_loop(0, breadth, force_edge, 0)

        source, target = first, second
        for sweep in range(1, SWEEPS):
            last = sweep == SWEEPS - 1

            def relax(x, y, source=source, target=target):
                centre, total = beside(source, x, y)
                cell = x * wide + y
                target[cell] = 0.2 * centre + (forced[cell] + total)

            def finish(x, y, source=source):
                centre, total = beside(source, x, y)
                cell = x * wide + y
                value = corr[cell] + (0.2 * centre + (forced[cell] + total))
                start = part * own + (x - 2) * breadth + y - 2
                out[pl.ds(start, rhs, stride=parts * own), :] = value

            def row(i, carry, last=last, relax=relax, finish=finish):
                if last:
                    for y in range(breadth):
                        finish(i + 2, y + 2)
                else:
                    for y in range(breadth + 2):
                        relax(i + 2, y + 1)
                return carry

            lax.fori_loop(0, depth, row, 0)
            if not last:
                def edge(i, carry, relax=relax):
                    relax(1, i + 2)
                    relax(depth + 2, i + 2)
                    return carry

                lax.fori_loop(0, breadth, edge, 0)
            source, target = target, source
        return carry

    lax.fori_loop(0, parts, component, 0)


def schwarz(residuals, vectors_ext, modulus_ext, grid, halo_x, halo_y):
    rhs, parts, depth, breadth, length = residuals.shape
    width = vectors_ext.shape[0]
    diagonal, west, east, south, north, lower, upper = face_weights(modulus_ext)
    inner = modulus_ext[1:-1, 1:-1, :]
    scale = jnp.where(inner > 0, 0.8, 0.0) / diagonal
    z = jnp.arange(length, dtype=jnp.int32)
    lower = jnp.where(z > 0, lower, 0.0)
    upper = jnp.where(z < length - 1, upper, 0.0)
    weights = jnp.stack(
        [scale] + [scale * w for w in (west, east, south, north, lower, upper)] + [jnp.zeros_like(scale)],
        axis=2,
    ).reshape((depth + 2) * (breadth + 2), 8, length)
    cells = (depth + 4) * (breadth + 4)
    vec = vectors_ext.transpose(1, 2, 3, 0, 4).reshape(parts, cells, width, length)
    vmem = pl.BlockSpec(memory_space=pltpu.VMEM)
    field = pltpu.VMEM((cells, rhs, length), jnp.float32)
    result = pl.pallas_call(
        functools.partial(schwarz_kernel, rhs, parts, depth, breadth, width),
        out_shape=jax.ShapeDtypeStruct((rhs * parts * depth * breadth, length), jnp.float32),
        in_specs=[vmem] * 6,
        out_specs=vmem,
        scratch_shapes=[pltpu.VMEM((9 * width, rhs, length), jnp.float32), field, field, field, field],
        compiler_params=pltpu.CompilerParams(vmem_limit_bytes=48 * 1024 * 1024),
    )(
        residuals.reshape(-1, length),
        vec,
        weights,
        grid.T,
        halo_x.reshape(-1, length),
        halo_y.reshape(-1, length),
    )
    return result.reshape(residuals.shape)


def on_device(residuals, vectors, phases, stiffness):
    count_x = lax.axis_size("gx")
    count_y = lax.axis_size("yz")
    position = lax.axis_index("gx") * count_y + lax.axis_index("yz")
    width = vectors.shape[0]
    levels = stiffness.shape[0]
    choose = (phases[None] == jnp.arange(levels, dtype=jnp.int32)[:, None, None, None]).astype(
        jnp.float32
    )
    modulus = jnp.sum(stiffness[:, None, None, None] * choose, axis=0)
    vectors_ext = extended(vectors, (("gx", 2), ("yz", 3)), 2)
    modulus_ext = extended(modulus[None, None], (("gx", 2), ("yz", 3)), 2)[0, 0]
    blocks = coarse_blocks(vectors_ext, modulus_ext)
    coarse_rhs = jnp.einsum("kcxyz,rcxyz->kr", vectors, residuals, precision=HIGH)
    panel = panel_row(blocks, coarse_rhs, count_y)
    coeffs_all, grid, halo_x, halo_y = coarse_solve(panel, residuals, count_x, count_y, width)
    coeffs = grid[4 * width : 5 * width]
    result = schwarz(residuals, vectors_ext, modulus_ext, grid, halo_x, halo_y)
    return (coeffs, result)


def solution(mesh):
    return jax.shard_map(
        on_device,
        mesh=mesh,
        in_specs=(
            P(None, None, "gx", "yz", None),
            P(None, None, "gx", "yz", None),
            P("gx", "yz", None),
            P(),
        ),
        out_specs=(P(("gx", "yz"), None), P(None, None, "gx", "yz", None)),
        check_vma=False,
    )
```

profile of v0, /device:TPU:9, one launch (start us, length us, event | category | flops | bytes accessed | tf_op | source)
XLA Modules:
  0.0 117.9 jit_solution(5146729132060946595)
XLA Ops:
  0.6 0.9 select_reduce_fusion
  1.6 3.1 %collective-permute-start = (f32[1,1,2,8,128]{4,3,2,1,0:T(8,128)S(1)}, f32[1,1,2,8,128]{4,3,2,1,0:T(8,128)S(1)}, u32[]{:S(2)}, u32[]{:S(2)}) collective-permute-start(f32[1,1,2,8,128]{4,3,2,1,0:T(8,128)S(1)} %get-tuple-element.34), channel_id=1, source_target_pairs={{0,4},{4,8},{8,12},{12,16},{16,20},{20,24},{24,28},{1,5},{5,9},{9,... | collective-permute-start | bytes 24584 | tf_op jit(solution)/shard_map/ppermute | solution.py:24
  4.7 3.1 %collective-permute-start.1 = (f32[1,1,2,8,128]{4,3,2,1,0:T(8,128)S(1)}, f32[1,1,2,8,128]{4,3,2,1,0:T(8,128)S(1)}, u32[]{:S(2)}, u32[]{:S(2)}) collective-permute-start(f32[1,1,2,8,128]{4,3,2,1,0:T(8,128)S(1)} %get-tuple-element.35), channel_id=1, source_target_pairs={{4,0},{8,4},{12,8},{16,12},{20,16},{24,20},{28,24},{5,1},{9,5},{13... | collective-permute-start | bytes 24584 | tf_op jit(solution)/shard_map/ppermute | solution.py:26
  7.8 1.1 fusion.58
  8.9 2.1 %collective-permute-start.5 = (f32[8,3,2,8,128]{4,0,2,1,3:T(8,128)S(1)}, f32[8,3,2,8,128]{4,0,2,1,3:T(8,128)S(1)}, u32[]{:S(2)}, u32[]{:S(2)}) collective-permute-start(f32[8,3,2,8,128]{4,0,2,1,3:T(8,128)S(1)} %copy.73), channel_id=1, source_target_pairs={{4,0},{8,4},{12,8},{16,12},{20,16},{24,20},{28,24},{5,1},{9,5},{13... | collective-permute-start | bytes 589832 | tf_op jit(solution)/shard_map/ppermute | solution.py:26
  11.1 3.2 %collective-permute-start.4 = (f32[8,3,2,8,128]{4,0,2,1,3:T(8,128)S(1)}, f32[8,3,2,8,128]{4,0,2,1,3:T(8,128)S(1)}, u32[]{:S(2)}, u32[]{:S(2)}) collective-permute-start(f32[8,3,2,8,128]{4,0,2,1,3:T(8,128)S(1)} %copy.74), channel_id=1, source_target_pairs={{0,4},{4,8},{8,12},{12,16},{16,20},{20,24},{24,28},{1,5},{5,9},{9,... | collective-permute-start | bytes 589832 | tf_op jit(solution)/shard_map/ppermute | solution.py:24
  14.3 6.7 %fusion.2 = f32[8,32]{1,0:T(8,128)} fusion(f32[32,3,8,8,128]{4,3,2,1,0:T(8,128)} %res.1, f32[8,3,8,8,128]{4,3,2,1,0:T(8,128)S(1)} %copy-done.2), kind=kOutput, calls=%fused_computation.10 | convolution fusion | flops 75497472 | bytes 3933184 | tf_op jit(solution)/shard_map/kcxyz,rcxyz->kr/dot_general | solution.py:453
  21.1 4.5 %fusion.56 = (f32[32,3,8,1,128]{4,3,2,1,0:T(1,128)}, f32[32,3,8,1,128]{4,3,2,1,0:T(1,128)}) fusion(f32[32,3,8,8,128]{4,3,2,1,0:T(8,128)} %res.1), kind=kLoop, calls=%fused_computation.104 | loop fusion | bytes 1572864 | tf_op jit(solution)/shard_map/slice | solution.py:263
  25.7 4.8 %collective-permute-start.2 = (f32[1,1,12,2,128]{4,3,2,1,0:T(2,128)S(1)}, f32[1,1,12,2,128]{4,3,2,1,0:T(2,128)S(1)}, u32[]{:S(2)}, u32[]{:S(2)}) collective-permute-start(f32[1,1,12,2,128]{4,3,2,1,0:T(2,128)S(1)} %get-tuple-element.32), channel_id=1, source_target_pairs={{0,1},{1,2},{2,3},{4,5},{5,6},{6,7},{8,9},{9,10},{10,11},{12,13},{... | collective-permute-start | bytes 36872 | tf_op jit(solution)/shard_map/ppermute | solution.py:24
  30.5 1.9 %collective-permute-start.3 = (f32[1,1,12,2,128]{4,3,2,1,0:T(2,128)S(1)}, f32[1,1,12,2,128]{4,3,2,1,0:T(2,128)S(1)}, u32[]{:S(2)}, u32[]{:S(2)}) collective-permute-start(f32[1,1,12,2,128]{4,3,2,1,0:T(2,128)S(1)} %get-tuple-element.33), channel_id=1, source_target_pairs={{1,0},{2,1},{3,2},{5,4},{6,5},{7,6},{9,8},{10,9},{11,10},{13,12},{... | collective-permute-start | bytes 36872 | tf_op jit(solution)/shard_map/ppermute | solution.py:26
  32.5 0.1 mul.302
  32.5 0.7 mul.303
  33.2 0.1 mul.292
  33.3 0.7 mul.293
  33.9 0.1 mul.282
  34.0 0.6 mul.283
  34.6 0.9 collective-permute-done.3
  35.6 0.1 select_multiply_fusion
  35.8 0.1 add_add_fusion
  36.0 0.1 fusion.41
  36.4 0.5 fusion.12
  36.9 2.3 %convolution_bitcast_fusion = f32[8,8]{0,1:T(8,128)S(1)} fusion(f32[8,3,8,8,128]{4,3,2,1,0:T(8,128)S(1)} %fusion.12, f32[8,3,8,8,128]{4,3,2,1,0:T(8,128)S(1)} %copy-done.2), kind=kOutput, calls=%fused_computation.9 | convolution fusion | flops 18874368 | bytes 1573120 | tf_op jit(solution)/shard_map/kcxyz,lcxyz->kl/dot_general | solution.py:62
  39.2 0.1 copy.26
  39.2 0.7 mul.281
  39.9 0.1 slice_multiply_fusion.1
  40.1 0.7 stack.31.weights
  40.8 0.5 constant_dynamic-update-slice_fusion.1
  41.4 2.7 %collective-permute-start.6 = (f32[8,3,12,2,128]{4,0,2,1,3:T(8,128)S(1)}, f32[8,3,12,2,128]{4,0,2,1,3:T(8,128)S(1)}, u32[]{:S(2)}, u32[]{:S(2)}) collective-permute-start(f32[8,3,12,2,128]{4,0,2,1,3:T(8,128)S(1)} %get-tuple-element.19), channel_id=1, source_target_pairs={{0,1},{1,2},{2,3},{4,5},{5,6},{6,7},{8,9},{9,10},{10,11},{12,13},{... | collective-permute-start | bytes 884744 | tf_op jit(solution)/shard_map/ppermute | solution.py:24
  44.2 2.1 %collective-permute-start.7 = (f32[8,3,12,2,128]{4,0,2,1,3:T(8,128)S(1)}, f32[8,3,12,2,128]{4,0,2,1,3:T(8,128)S(1)}, u32[]{:S(2)}, u32[]{:S(2)}) collective-permute-start(f32[8,3,12,2,128]{4,0,2,1,3:T(8,128)S(1)} %get-tuple-element.20), channel_id=1, source_target_pairs={{1,0},{2,1},{3,2},{5,4},{6,5},{7,6},{9,8},{10,9},{11,10},{13,12},{... | collective-permute-start | bytes 884744 | tf_op jit(solution)/shard_map/ppermute | solution.py:26
  46.3 0.3 fusion.5
  46.6 0.3 fusion.6
  46.9 0.1 mul.318
  47.0 0.1 mul.311
  47.1 0.7 collective-permute-done.6
  47.8 0.3 fusion.8
  48.1 0.1 mul.291
  48.2 4.0 %collective-permute-done.7 = f32[8,3,12,2,128]{4,0,2,1,3:T(8,128)S(1)} collective-permute-done((f32[8,3,12,2,128]{4,0,2,1,3:T(8,128)S(1)}, f32[8,3,12,2,128]{4,0,2,1,3:T(8,128)S(1)}, u32[]{:S(2)}, u32[]{:S(2)}) %collective-permute-start.7) | collective-permute-done | bytes 294944 | tf_op jit(solution)/shard_map/ppermute | solution.py:26
  52.2 0.3 fusion.7
  52.5 0.1 mul.301
  52.7 0.7 pad_maximum_fusion.3.panel
  53.4 24.9 %shard_map.59 = (f32[256,32]{1,0:T(8,128)}, f32[72,32]{1,0:T(8,128)}, f32[2,32,3,8,128]{4,3,2,1,0:T(8,128)}, f32[2,32,3,8,128]{4,3,2,1,0:T(8,128)}) custom-call(f32[8,128]{1,0:T(8,128)} %pad_maximum_fusion.3.panel, f32[32,3,8,8,128]{4,3,2,1,0:T(8,128)} %res.1, f32[32,3,8,128]{3,2,1,0:T(8,128)} %bitcast.84, f32[32,3,8,128]{3,2,1,0:T(8,128)} %bitcast.83), custom_call_target="tpu_custom_call" | custom-call | tf_op jit(solution)/shard_map/pallas_call | solution.py:245
  78.3 1.3 %slice.172 = f32[8,32]{1,0:T(8,128)} slice(f32[72,32]{1,0:T(8,128)} %get-tuple-element.5), slice={[32:40], [0:32]} | slice | bytes 2048 | tf_op jit(solution)/shard_map/slice | solution.py:456
  79.5 0.8 copy.41
  80.4 0.1 maximum_bitcast_fusion
  80.5 0.2 copy.40
  80.8 0.9 copy-done
  81.6 0.2 copy-done.1
  81.9 36.0 %shard_map.60 = f32[6144,128]{1,0:T(8,128)} custom-call(f32[6144,128]{1,0:T(8,128)} %bitcast.81, f32[3,144,8,128]{3,2,1,0:T(8,128)S(1)} %bitcast.77, f32[100,8,128]{2,1,0:T(8,128)S(1)} %stack.31.weights, f32[32,72]{1,0:T(8,128)S(1)} %bitcast.80, f32[1536,128]{1,0:T(8,128)S(1)} %bitcast.78, f32[1536,128]{1,0:T(8,128)S(1)} %bitcast.79), custom_call_target="tpu_custom_call" | custom-call | tf_op jit(solution)/shard_map/pallas_call | solution.py:422
  (52 shorter events, 0.8 us)
Async XLA Ops:
  0.6 13.7 %copy-start.2 = (f32[8,3,8,8,128]{4,3,2,1,0:T(8,128)S(1)}, f32[8,3,8,8,128]{4,3,2,1,0:T(8,128)}, u32[]{:S(2)}) copy-start(f32[8,3,8,8,128]{4,3,2,1,0:T(8,128)} %param.5) | copy-start | bytes 2359300
  1.6 24.0 %collective-permute-start = (f32[1,1,2,8,128]{4,3,2,1,0:T(8,128)S(1)}, f32[1,1,2,8,128]{4,3,2,1,0:T(8,128)S(1)}, u32[]{:S(2)}, u32[]{:S(2)}) collective-permute-start(f32[1,1,2,8,128]{4,3,2,1,0:T(8,128)S(1)} %get-tuple-element.34), channel_id=1, source_target_pairs={{0,4},{4,8},{8,12},{12,16},{16,20},{20,24},{24,28},{1,5},{5,9},{9,... | collective-permute-start | bytes 24584 | tf_op jit(solution)/shard_map/ppermute | solution.py:24
  4.7 20.9 %collective-permute-start.1 = (f32[1,1,2,8,128]{4,3,2,1,0:T(8,128)S(1)}, f32[1,1,2,8,128]{4,3,2,1,0:T(8,128)S(1)}, u32[]{:S(2)}, u32[]{:S(2)}) collective-permute-start(f32[1,1,2,8,128]{4,3,2,1,0:T(8,128)S(1)} %get-tuple-element.35), channel_id=1, source_target_pairs={{4,0},{8,4},{12,8},{16,12},{20,16},{24,20},{28,24},{5,1},{9,5},{13... | collective-permute-start | bytes 24584 | tf_op jit(solution)/shard_map/ppermute | solution.py:26
  8.9 32.4 %collective-permute-start.5 = (f32[8,3,2,8,128]{4,0,2,1,3:T(8,128)S(1)}, f32[8,3,2,8,128]{4,0,2,1,3:T(8,128)S(1)}, u32[]{:S(2)}, u32[]{:S(2)}) collective-permute-start(f32[8,3,2,8,128]{4,0,2,1,3:T(8,128)S(1)} %copy.73), channel_id=1, source_target_pairs={{4,0},{8,4},{12,8},{16,12},{20,16},{24,20},{28,24},{5,1},{9,5},{13... | collective-permute-start | bytes 589832 | tf_op jit(solution)/shard_map/ppermute | solution.py:26
  11.1 29.7 %collective-permute-start.4 = (f32[8,3,2,8,128]{4,0,2,1,3:T(8,128)S(1)}, f32[8,3,2,8,128]{4,0,2,1,3:T(8,128)S(1)}, u32[]{:S(2)}, u32[]{:S(2)}) collective-permute-start(f32[8,3,2,8,128]{4,0,2,1,3:T(8,128)S(1)} %copy.74), channel_id=1, source_target_pairs={{0,4},{4,8},{8,12},{12,16},{16,20},{20,24},{24,28},{1,5},{5,9},{9,... | collective-permute-start | bytes 589832 | tf_op jit(solution)/shard_map/ppermute | solution.py:24
  25.7 8.9 %collective-permute-start.2 = (f32[1,1,12,2,128]{4,3,2,1,0:T(2,128)S(1)}, f32[1,1,12,2,128]{4,3,2,1,0:T(2,128)S(1)}, u32[]{:S(2)}, u32[]{:S(2)}) collective-permute-start(f32[1,1,12,2,128]{4,3,2,1,0:T(2,128)S(1)} %get-tuple-element.32), channel_id=1, source_target_pairs={{0,1},{1,2},{2,3},{4,5},{5,6},{6,7},{8,9},{9,10},{10,11},{12,13},{... | collective-permute-start | bytes 36872 | tf_op jit(solution)/shard_map/ppermute | solution.py:24
  30.5 5.0 %collective-permute-start.3 = (f32[1,1,12,2,128]{4,3,2,1,0:T(2,128)S(1)}, f32[1,1,12,2,128]{4,3,2,1,0:T(2,128)S(1)}, u32[]{:S(2)}, u32[]{:S(2)}) collective-permute-start(f32[1,1,12,2,128]{4,3,2,1,0:T(2,128)S(1)} %get-tuple-element.33), channel_id=1, source_target_pairs={{1,0},{2,1},{3,2},{5,4},{6,5},{7,6},{9,8},{10,9},{11,10},{13,12},{... | collective-permute-start | bytes 36872 | tf_op jit(solution)/shard_map/ppermute | solution.py:26
  41.3 11.3 %copy-start.4 = (f32[8,32]{1,0:T(8,128)S(1)}, f32[8,32]{1,0:T(8,128)}, u32[]{:S(2)}) copy-start(f32[8,32]{1,0:T(8,128)} %mul.281) | copy-start | bytes 3076
  41.3 11.3 %copy-start.5 = (f32[32]{0:T(128)S(1)}, f32[32]{0:T(128)}, u32[]{:S(2)}) copy-start(f32[32]{0:T(128)} %mul.303) | copy-start | bytes 388
  41.3 11.3 %copy-start.6 = (f32[32]{0:T(128)S(1)}, f32[32]{0:T(128)}, u32[]{:S(2)}) copy-start(f32[32]{0:T(128)} %mul.293) | copy-start | bytes 388
  41.3 11.3 %copy-start.7 = (f32[32]{0:T(128)S(1)}, f32[32]{0:T(128)}, u32[]{:S(2)}) copy-start(f32[32]{0:T(128)} %mul.283) | copy-start | bytes 388
  41.3 11.3 %copy-start.3 = (f32[8,32]{1,0:T(8,128)S(1)}, f32[8,32]{1,0:T(8,128)}, u32[]{:S(2)}) copy-start(f32[8,32]{1,0:T(8,128)} %fusion.2) | copy-start | bytes 3076
  41.4 6.4 %collective-permute-start.6 = (f32[8,3,12,2,128]{4,0,2,1,3:T(8,128)S(1)}, f32[8,3,12,2,128]{4,0,2,1,3:T(8,128)S(1)}, u32[]{:S(2)}, u32[]{:S(2)}) collective-permute-start(f32[8,3,12,2,128]{4,0,2,1,3:T(8,128)S(1)} %get-tuple-element.19), channel_id=1, source_target_pairs={{0,1},{1,2},{2,3},{4,5},{5,6},{6,7},{8,9},{9,10},{10,11},{12,13},{... | collective-permute-start | bytes 884744 | tf_op jit(solution)/shard_map/ppermute | solution.py:24
  44.2 8.0 %collective-permute-start.7 = (f32[8,3,12,2,128]{4,0,2,1,3:T(8,128)S(1)}, f32[8,3,12,2,128]{4,0,2,1,3:T(8,128)S(1)}, u32[]{:S(2)}, u32[]{:S(2)}) collective-permute-start(f32[8,3,12,2,128]{4,0,2,1,3:T(8,128)S(1)} %get-tuple-element.20), channel_id=1, source_target_pairs={{1,0},{2,1},{3,2},{5,4},{6,5},{7,6},{9,8},{10,9},{11,10},{13,12},{... | collective-permute-start | bytes 884744 | tf_op jit(solution)/shard_map/ppermute | solution.py:26
  80.5 1.1 copy-start
  80.5 1.4 %copy-start.1 = (f32[2,32,3,8,128]{4,3,2,1,0:T(8,128)S(1)}, f32[2,32,3,8,128]{4,3,2,1,0:T(8,128)}, u32[]{:S(2)}) copy-start(f32[2,32,3,8,128]{4,3,2,1,0:T(8,128)} %get-tuple-element.7) | copy-start | bytes 2359300
where the time goes:
time: 119 us; the launch traced here: 118 us
  Pallas kernels  60.9 us (51%)
  starting transfers between devices  23.1 us (19%)
  local copies, waits for them, and re-layouts  14.3 us (12%)
  matrix products  10.1 us (8%)
  waiting for transfers between devices  5.63 us (5%)
  other arithmetic  2.79 us (2%)
    pallas_call x1, Pallas kernels, schwarz(): pl.pallas_call(functools.partial(schwarz_kernel, rhs, parts, depth, bread...  36 us
    pallas_call x1, Pallas kernels, coarse_solve(): pl.pallas_call(functools.partial(coarse_kernel, count_x, count_y, width),...  24.9 us
    ppermute x4, starting transfers between devices, extended(): lax.ppermute(tail, axis, [(i, (i + 1) % count) for i in range(ends)])  13.9 us
    ppermute x4, starting transfers between devices, extended(): lax.ppermute(head, axis, [((i + 1) % count, i) for i in range(ends)])  9.19 us
    dot_general x1, matrix products, on_device(): jnp.einsum('kcxyz,rcxyz->kr', vectors, residuals, precision=HIGH)  6.73 us
    ppermute x4, waiting for transfers between devices, extended(): lax.ppermute(head, axis, [((i + 1) % count, i) for i in range(ends)])  4.9 us
    slice x1, local copies, waits for them, and re-layouts, coarse_solve(): residuals[:, :, :, -1, :]  4.55 us
    mul x16, local copies, waits for them, and re-layouts, placed(): block[:, None, :] * select[None, :, None]  3.37 us
  transfers between devices with their start and end apart: 8, of which 3 were waited for; matrix products, arithmetic and copies ran while one was open for 18% of the time, Pallas kernels for 0%

commit v1 on v0

v1 whole, which is shorter than its diff:
```python
import functools

import jax
import jax.numpy as jnp
from jax import lax
from jax.experimental import pallas as pl
from jax.experimental.pallas import tpu as pltpu
from jax.sharding import PartitionSpec as P

SWEEPS = 4


HIGH = lax.Precision.HIGHEST


MESH = pl.DeviceIdType.MESH


def eliminate(rows, size):
    sublane = lax.broadcasted_iota(jnp.int32, rows[0].shape, 0)
    for p in range(size):
        reduced = []
        for a in rows:
            column = jnp.broadcast_to(a[:, p : p + 1], a.shape)
            pivot = a[p : p + 1, :] / column[p : p + 1, :]
            reduced.append(jnp.where(sublane == p, pivot, a - column * pivot))
        rows = reduced
    return rows


def product(a, b):
    return jnp.dot(a, b, precision=HIGH, preferred_element_type=jnp.float32)


def cyclic_solve(rows, size):
    count = len(rows)
    width = rows[0].shape[1]
    lane = lax.broadcasted_iota(jnp.int32, rows[0].shape, 1)
    is_own = lane < size
    is_low = (lane >= size) & (lane < 2 * size)
    is_high = (lane >= 2 * size) & (lane < 3 * size)
    is_rhs = lane >= 3 * size
    live = list(range(count))
    system = dict(enumerate(rows))
    levels = []
    while len(live) > 1:
        out = live[1::2]
        kept = live[0::2]
        solved = dict(zip(out, eliminate([system[i] for i in out], size)))
        fresh = {}
        for place, i in enumerate(kept):
            a = system[i]
            total = jnp.where(is_own | is_rhs, a, 0.0)
            if place > 0:
                t = product(a[:, size : 2 * size], solved[out[place - 1]])
                shifted = pltpu.roll(t, width - 2 * size, 1)
                total = total - jnp.where(is_own, shifted, jnp.where(is_low | is_rhs, t, 0.0))
            if place < len(out):
                t = product(a[:, 2 * size : 3 * size], solved[out[place]])
                shifted = pltpu.roll(t, width - size, 1)
                total = total - jnp.where(is_own, shifted, jnp.where(is_high | is_rhs, t, 0.0))
            fresh[i] = total
        levels.append((live, out, solved))
        system = fresh
        live = kept
    last = eliminate([system[live[0]]], size)[0]
    answer = {live[0]: last[:, 3 * size :]}
    for before, out, solved in reversed(levels):
        for i in out:
            a = solved[i]
            place = before.index(i)
            x = a[:, 3 * size :] - product(a[:, size : 2 * size], answer[before[place - 1]])
            if place + 1 < len(before):
                x = x - product(a[:, 2 * size : 3 * size], answer[before[place + 1]])
            answer[i] = x
    return [answer[i] for i in range(count)]


def cell_weights(ext, x, y):
    field = ext.shape[0] - 1
    m = ext[field, x, y]
    length = m.shape[1]
    z = lax.broadcasted_iota(jnp.int32, m.shape, 1)
    low = 0.5 * (m + jnp.where(z > 0, pltpu.roll(m, 1, 1), 0.0))
    high = 0.5 * (m + jnp.where(z < length - 1, pltpu.roll(m, length - 1, 1), 0.0))
    west = 0.5 * (m + ext[field, x - 1, y])
    east = 0.5 * (m + ext[field, x + 1, y])
    south = 0.5 * (m + ext[field, x, y - 1])
    north = 0.5 * (m + ext[field, x, y + 1])
    diagonal = 0.002 + west + east + south + north + low + high
    return m, diagonal, (
        west, east, south, north, jnp.where(z > 0, low, 0.0), jnp.where(z < length - 1, high, 0.0)
    )


def coarse_kernel(
    count_x, count_y, width, own, flat, res, south_face, north_face,
    coeffs, grid, halo_x, halo_y, ext,
    panel, gathered, send_sem, recv_sem, halo_send, halo_recv
):
    index_x = lax.axis_index("gx")
    index_y = lax.axis_index("yz")
    count = count_x * count_y
    me = index_x * count_y + index_y
    fields, depth, breadth = own.shape[:3]
    parts = fields - 1
    rhs = res.shape[0]
    length = own.shape[4]
    barrier = pltpu.get_barrier_semaphore()
    zero = jnp.zeros((width, length), jnp.float32)

    def clear(x, carry):
        for f in range(fields):
            for y in range(breadth + 4):
                ext[f, x, y] = zero
        return carry

    lax.fori_loop(0, depth + 4, clear, 0)

    def fill(x, carry):
        for f in range(fields):
            for y in range(breadth):
                ext[f, x + 2, y + 2] = own[f, x, y]
        return carry

    lax.fori_loop(0, depth, fill, 0)

    def greet(step, carry):
        other = lax.rem(me + step, count)
        pl.semaphore_signal(
            barrier, inc=1, device_id=(other // count_y, lax.rem(other, count_y)), device_id_type=MESH
        )
        return carry

    lax.fori_loop(1, count, greet, 0)
    pl.semaphore_wait(barrier, count - 1)

    def can(dx, dy):
        ok = index_x >= 0
        if dx:
            ok = index_x > 0 if dx < 0 else index_x < count_x - 1
        if dy:
            ok_y = index_y > 0 if dy < 0 else index_y < count_y - 1
            ok = jnp.logical_and(ok, ok_y) if dx else ok_y
        return ok

    started = []

    def start(source, target, dx, dy):
        slot = len(started)
        copy = pltpu.make_async_remote_copy(
            src_ref=source,
            dst_ref=target,
            send_sem=halo_send.at[slot],
            recv_sem=halo_recv.at[slot],
            device_id=(index_x + dx, index_y + dy),
            device_id_type=MESH,
        )
        pl.when(can(dx, dy))(copy.start)
        started.append((can(dx, dy), can(-dx, -dy), copy))

    def layer(step):
        inner_x, inner_y = pl.ds(2, depth), pl.ds(2, breadth)
        start(own.at[:, step], ext.at[:, depth + 2 + step, inner_y], -1, 0)
        start(own.at[:, depth - 1 - step], ext.at[:, 1 - step, inner_y], 1, 0)
        start(own.at[:, :, step], ext.at[:, inner_x, breadth + 2 + step], 0, -1)
        start(own.at[:, :, breadth - 1 - step], ext.at[:, inner_x, 1 - step], 0, 1)

    layer(0)
    cells = depth * breadth

    def loads(i, sums):
        f = i // cells
        cell = i - f * cells
        v = own[f, cell // breadth, lax.rem(cell, breadth)]
        return tuple(
            total + v * flat[pl.ds(r * parts * cells + i, 1), :] for r, total in enumerate(sums)
        )

    sums = lax.fori_loop(0, parts * cells, loads, (zero,) * rhs)
    lane = lax.broadcasted_iota(jnp.int32, panel.shape, 1)

    def placed(total, at):
        return jnp.where(lane == at, jnp.sum(total, axis=1, keepdims=True), 0.0)

    size = count_y * width
    row = jnp.zeros(panel.shape, jnp.float32)
    for r in range(rhs):
        row = row + placed(sums[r], 3 * size + r)
    for _, receives, copy in started:
        pl.when(receives)(copy.wait_recv)

    def gram(sums, left, f, x, y):
        return tuple(
            total + left * ext[f, x, y, pl.ds(l, 1), :] for l, total in enumerate(sums)
        )

    def own_block(i, sums):
        inside_x = (
            jnp.where(i > 0, 1.0, 0.0).astype(jnp.float32),
            jnp.where(i < depth - 1, 1.0, 0.0).astype(jnp.float32),
        )
        x = i + 2
        for y in range(2, breadth + 2):
            _, diagonal, (west, east, south, north, low, high) = cell_weights(ext, x, y)
            west = west * inside_x[0]
            east = east * inside_x[1]
            for f in range(parts):
                v = ext[f, x, y]
                near = west * ext[f, x - 1, y] + east * ext[f, x + 1, y]
                if y > 2:
                    near = near + south * ext[f, x, y - 1]
                if y < breadth + 1:
                    near = near + north * ext[f, x, y + 1]
                near = near + low * pltpu.roll(v, 1, 1) + high * pltpu.roll(v, length - 1, 1)
                sums = gram(sums, diagonal * v - near, f, x, y)
        return sums

    def side_block(along, fixed_x, fixed_y, dx, dy):
        which = {(-1, 0): 0, (1, 0): 1, (0, -1): 2, (0, 1): 3}[(dx, dy)]

        def one(i, sums):
            x = i + 2 if fixed_x is None else fixed_x
            y = i + 2 if fixed_y is None else fixed_y
            weight = cell_weights(ext, x, y)[2][which]
            for f in range(parts):
                sums = gram(sums, -weight * ext[f, x, y], f, x + dx, y + dy)
            return sums

        return lax.fori_loop(0, along, one, (zero,) * width)

    blocks = (
        (lax.fori_loop(0, depth, own_block, (zero,) * width), index_y * width),
        (side_block(depth, None, 2, 0, -1), (index_y - 1) * width),
        (side_block(depth, None, breadth + 1, 0, 1), (index_y + 1) * width),
        (side_block(breadth, 2, None, -1, 0), size + index_y * width),
        (side_block(breadth, depth + 1, None, 1, 0), 2 * size + index_y * width),
    )
    for totals, at in blocks:
        for l in range(width):
            row = row + placed(totals[l], at + l)
    panel[...] = row
    gathered[me] = row

    def sending(other, slot):
        return pltpu.make_async_remote_copy(
            src_ref=panel,
            dst_ref=gathered.at[slot],
            send_sem=send_sem.at[other],
            recv_sem=recv_sem.at[slot],
            device_id=(other // count_y, lax.rem(other, count_y)),
            device_id_type=MESH,
        )

    def send(step, carry):
        sending(lax.rem(me + step, count), me).start()
        return carry

    lax.fori_loop(1, count, send, 0)
    first = len(started)
    layer(1)
    ends_x = ((0, -1, depth + 2), (depth - 1, 1, 1))
    ends_y = ((0, -1, breadth + 2), (breadth - 1, 1, 1))
    for x, dx, to_x in ends_x:
        for y, dy, to_y in ends_y:
            start(own.at[:, x, y], ext.at[:, to_x, to_y], dx, dy)
    start(res.at[:, :, 0], halo_x.at[1], -1, 0)
    start(res.at[:, :, depth - 1], halo_x.at[0], 1, 0)
    start(south_face, halo_y.at[1], 0, -1)
    start(north_face, halo_y.at[0], 0, 1)

    def collect(step, carry):
        other = lax.rem(me + step, count)
        sending(other, other).wait_recv()
        return carry

    lax.fori_loop(1, count, collect, 0)
    rows = [gathered[pl.ds(g * count_y, count_y)].reshape(size, length) for g in range(count_x)]
    for g, x in enumerate(cyclic_solve(rows, size)):
        coeffs[pl.ds(g * size, size), :] = x
    slot = 0
    for step_x in (-1, 0, 1):
        for step_y in (-1, 0, 1):
            near_x = jnp.clip(index_x + step_x, 0, count_x - 1)
            near_y = jnp.clip(index_y + step_y, 0, count_y - 1)
            begin = pl.multiple_of((near_x * count_y + near_y) * width, width)
            grid[pl.ds(slot * width, width), :] = coeffs[pl.ds(begin, width), :]
            slot += 1

    def drain(step, carry):
        sending(lax.rem(me + step, count), me).wait_send()
        return carry

    lax.fori_loop(1, count, drain, 0)
    for place, (sends, receives, copy) in enumerate(started):
        pl.when(sends)(copy.wait_send)
        if place >= first:
            pl.when(receives)(copy.wait_recv)


def coarse_solve(own, residuals, count_x, count_y):
    rhs, parts, depth, breadth, length = residuals.shape
    fields, width = own.shape[0], own.shape[3]
    count = count_x * count_y
    vmem = pl.BlockSpec(memory_space=pltpu.VMEM)
    hbm = pl.BlockSpec(memory_space=pl.ANY)
    panel = (width, 3 * count_y * width + rhs)
    return pl.pallas_call(
        functools.partial(coarse_kernel, count_x, count_y, width),
        out_shape=(
            jax.ShapeDtypeStruct((count * width, rhs), jnp.float32),
            jax.ShapeDtypeStruct((9 * width, rhs), jnp.float32),
            jax.ShapeDtypeStruct((2, rhs, parts, breadth, length), jnp.float32),
            jax.ShapeDtypeStruct((2, rhs, parts, depth, length), jnp.float32),
            jax.ShapeDtypeStruct((fields, depth + 4, breadth + 4, width, length), jnp.float32),
        ),
        in_specs=[vmem, vmem, hbm, hbm, hbm],
        out_specs=(vmem, vmem, hbm, hbm, vmem),
        scratch_shapes=[
            pltpu.VMEM(panel, jnp.float32),
            pltpu.VMEM((count,) + panel, jnp.float32),
            pltpu.SemaphoreType.DMA((count,)),
            pltpu.SemaphoreType.DMA((count,)),
            pltpu.SemaphoreType.DMA((16,)),
            pltpu.SemaphoreType.DMA((16,)),
        ],
        compiler_params=pltpu.CompilerParams(collective_id=0, has_side_effects=True),
    )(
        own,
        residuals.reshape(-1, length),
        residuals,
        residuals[:, :, :, 0, :],
        residuals[:, :, :, -1, :],
    )


def schwarz_kernel(
    rhs, parts, depth, breadth, width, res, ext, cgrid, halo_x, halo_y, out,
    weights, coeff, corr, forced, first, second
):
    length = res.shape[1]
    wide = breadth + 4
    own = depth * breadth

    for cls in range(9):
        for k in range(width):
            coeff[cls * width + k] = jnp.broadcast_to(
                cgrid[:, cls * width + k : cls * width + k + 1], (rhs, length)
            )
    zero = jnp.zeros((rhs, length), jnp.float32)
    for buffer in (first, second):
        def clear(i, carry, buffer=buffer):
            buffer[i] = zero
            return carry

        lax.fori_loop(0, (depth + 4) * wide, clear, 0)

    def weigh(i, carry):
        x = i // (breadth + 2) + 1
        y = lax.rem(i, breadth + 2) + 1
        m, diagonal, faces = cell_weights(ext, x, y)
        scale = jnp.where(m > 0, 0.8, 0.0) / diagonal
        weights[i, 0] = scale
        for q, w in enumerate(faces):
            weights[i, q + 1] = scale * w
        return carry

    lax.fori_loop(0, (depth + 2) * (breadth + 2), weigh, 0)

    def spread(w, q):
        return jnp.concatenate([weights[w, q]] * (rhs // width), axis=0)

    def component(part, carry):
        def region(cls, x0, nx, y0, ny):
            def one(i, carry):
                x = x0 + i // ny
                y = y0 + lax.rem(i, ny)
                value = coeff[cls * width] * ext[part, x, y, pl.ds(0, 1), :]
                for k in range(1, width):
                    value = value + coeff[cls * width + k] * ext[part, x, y, pl.ds(k, 1), :]
                corr[x * wide + y] = value
                return carry

            lax.fori_loop(0, nx * ny, one, 0, unroll=2 if nx * ny > 1 else 1)

        spans_x = ((0, 2), (2, depth), (depth + 2, 2))
        spans_y = ((0, 2), (2, breadth), (breadth + 2, 2))
        for a, (x0, nx) in enumerate(spans_x):
            for b, (y0, ny) in enumerate(spans_y):
                if a != 1 and b != 1:
                    region(a * 3 + b, 1 if a == 0 else x0, 1, 1 if b == 0 else y0, 1)
                else:
                    region(a * 3 + b, x0, nx, y0, ny)

        def beside(buffer, x, y):
            cell = x * wide + y
            w = (x - 1) * (breadth + 2) + y - 1
            centre = buffer[cell]
            total = spread(w, 1) * buffer[cell - wide]
            total = total + spread(w, 2) * buffer[cell + wide]
            total = total + spread(w, 3) * buffer[cell - 1]
            total = total + spread(w, 4) * buffer[cell + 1]
            total = total + spread(w, 5) * pltpu.roll(centre, 1, 1)
            total = total + spread(w, 6) * pltpu.roll(centre, length - 1, 1)
            return centre, total

        def force(x, y, loaded, outer):
            cell = x * wide + y
            w = (x - 1) * (breadth + 2) + y - 1
            centre, total = beside(corr, x, y)
            scale = spread(w, 0)
            term = scale * loaded
            if outer:
                term = jnp.where(scale > 0, term, 0.0)
            value = term - 0.8 * centre + total
            forced[cell] = value
            first[cell] = value

        def force_row(i, carry):
            for y in range(breadth):
                start = part * own + i * breadth + y
                force(i + 2, y + 2, res[pl.ds(start, rhs, stride=parts * own), :], False)
            for side in range(2):
                start = side * rhs * parts * depth + part * depth + i
                loaded = halo_y[pl.ds(start, rhs, stride=parts * depth), :]
                force(i + 2, 1 + side * (breadth + 1), loaded, True)
            return carry

        lax.fori_loop(0, depth, force_row, 0)

        def force_edge(i, carry):
            for side in range(2):
                start = side * rhs * parts * breadth + part * breadth + i
                loaded = halo_x[pl.ds(start, rhs, stride=parts * breadth), :]
                force(1 + side * (depth + 1), i + 2, loaded, True)
            return carry

        lax.fori_loop(0, breadth, force_edge, 0)

        source, target = first, second
        for sweep in range(1, SWEEPS):
            last = sweep == SWEEPS - 1

            def relax(x, y, source=source, target=target):
                centre, total = beside(source, x, y)
                cell = x * wide + y
                target[cell] = 0.2 * centre + (forced[cell] + total)

            def finish(x, y, source=source):
                centre, total = beside(source, x, y)
                cell = x * wide + y
                value = corr[cell] + (0.2 * centre + (forced[cell] + total))
                start = part * own + (x - 2) * breadth + y - 2
                out[pl.ds(start, rhs, stride=parts * own), :] = value

            def row(i, carry, last=last, relax=relax, finish=finish):
                if last:
                    for y in range(breadth):
                        finish(i + 2, y + 2)
                else:
                    for y in range(breadth + 2):
                        relax(i + 2, y + 1)
                return carry

            lax.fori_loop(0, depth, row, 0)
            if not last:
                def edge(i, carry, relax=relax):
                    relax(1, i + 2)
                    relax(depth + 2, i + 2)
                    return carry

                lax.fori_loop(0, breadth, edge, 0)
            source, target = target, source
        return carry

    lax.fori_loop(0, parts, component, 0)


def schwarz(residuals, ext, grid, halo_x, halo_y):
    rhs, parts, depth, breadth, length = residuals.shape
    width = ext.shape[3]
    vmem = pl.BlockSpec(memory_space=pltpu.VMEM)
    field = pltpu.VMEM(((depth + 4) * (breadth + 4), rhs, length), jnp.float32)
    result = pl.pallas_call(
        functools.partial(schwarz_kernel, rhs, parts, depth, breadth, width),
        out_shape=jax.ShapeDtypeStruct((rhs * parts * depth * breadth, length), jnp.float32),
        in_specs=[vmem] * 5,
        out_specs=vmem,
        scratch_shapes=[
            pltpu.VMEM(((depth + 2) * (breadth + 2), 7, width, length), jnp.float32),
            pltpu.VMEM((9 * width, rhs, length), jnp.float32),
            field, field, field, field,
        ],
        compiler_params=pltpu.CompilerParams(vmem_limit_bytes=48 * 1024 * 1024),
    )(
        residuals.reshape(-1, length),
        ext,
        grid.T,
        halo_x.reshape(-1, length),
        halo_y.reshape(-1, length),
    )
    return result.reshape(residuals.shape)


def on_device(residuals, vectors, phases, stiffness):
    count_x = lax.axis_size("gx")
    count_y = lax.axis_size("yz")
    width = vectors.shape[0]
    levels = stiffness.shape[0]
    choose = (phases[None] == jnp.arange(levels, dtype=jnp.int32)[:, None, None, None]).astype(
        jnp.float32
    )
    modulus = jnp.sum(stiffness[:, None, None, None] * choose, axis=0)
    spread = jnp.broadcast_to(modulus[None, :, :, None, :], (1,) + modulus.shape[:2] + (width, modulus.shape[2]))
    own = jnp.concatenate([vectors.transpose(1, 2, 3, 0, 4), spread], axis=0)
    coeffs_all, grid, halo_x, halo_y, ext = coarse_solve(own, residuals, count_x, count_y)
    coeffs = grid[4 * width : 5 * width]
    result = schwarz(residuals, ext, grid, halo_x, halo_y)
    return (coeffs, result)


def solution(mesh):
    return jax.shard_map(
        on_device,
        mesh=mesh,
        in_specs=(
            P(None, None, "gx", "yz", None),
            P(None, None, "gx", "yz", None),
            P("gx", "yz", None),
            P(),
        ),
        out_specs=(P(("gx", "yz"), None), P(None, None, "gx", "yz", None)),
        check_vma=False,
    )
```

time: 119 us -> 106 us (0.89)
  Pallas kernels: 60.9 us -> 90.9 us
  starting transfers between devices: 23.1 us -> 0 us
  matrix products: 10.1 us -> 0 us
  waiting for transfers between devices: 5.63 us -> 0 us
  local copies, waits for them, and re-layouts: 14.3 us -> 12.2 us
    ppermute x8 -> x0, starting transfers between devices: 23.1 us -> none  [the longest x4 13.9 us: extended(): lax.ppermute(tail, axis, [(i, (i + 1) % count) for i in range(ends)])]
    pallas_call x1, Pallas kernels: 24.9 us -> 46.1 us  [coarse_solve(): pl.pallas_call(functools.partial(coarse_kernel, count_x, count_y, width),...]
    dot_general x6 -> x0, matrix products: 10.1 us -> none  [the longest x1 6.73 us: on_device(): jnp.einsum('kcxyz,rcxyz->kr', vectors, residuals, precision=HIGH)]
    pallas_call x1, Pallas kernels: 36 us -> 44.7 us  [schwarz(): pl.pallas_call(functools.partial(schwarz_kernel, rhs, parts, depth, bread...]
    ppermute x8 -> x0, waiting for transfers between devices: 5.63 us -> none  [the longest x4 4.9 us: extended(): lax.ppermute(head, axis, [((i + 1) % count, i) for i in range(ends)])]
    unnamed x20 -> x7, local copies, waits for them, and re-layouts: 1.78 us -> 5.54 us
    mul x17 -> x0, local copies, waits for them, and re-layouts: 3.38 us -> none  [the longest x16 3.37 us: placed(): block[:, None, :] * select[None, :, None]]
  transfers between devices with their start and end apart: 8 -> 0, of which waited for: 3 -> 0; matrix products, arithmetic and copies ran while one was open for 18% -> 0% of each run, Pallas kernels for 0% -> 0%
where the time goes in v1:
time: 106 us
  Pallas kernels  90.9 us (86%)
  local copies, waits for them, and re-layouts  12.2 us (12%)
  other arithmetic  1.95 us (2%)
    pallas_call x1, Pallas kernels, coarse_solve(): pl.pallas_call(functools.partial(coarse_kernel, count_x, count_y, width),...  46.1 us
    pallas_call x1, Pallas kernels, schwarz(): pl.pallas_call(functools.partial(schwarz_kernel, rhs, parts, depth, bread...  44.7 us
    unnamed x7, local copies, waits for them, and re-layouts  5.54 us
    slice x1, local copies, waits for them, and re-layouts, coarse_solve(): residuals[:, :, :, -1, :]  4.57 us

profile of v1, /device:TPU:9, one launch (start us, length us, event | category | flops | bytes accessed | tf_op | source)
XLA Modules:
  0.0 105.7 jit_solution(4378307160218022232)
XLA Ops:
  0.6 0.9 select_reduce_fusion
  1.5 1.6 %copy.17 = f32[8,3,8,8,128]{4,0,3,2,1:T(8,128)S(1)} copy(f32[8,3,8,8,128]{4,3,2,1,0:T(8,128)} %param.5) | data formatting | bytes 1572864 | tf_op args[1]
  3.1 1.1 %pad_maximum_fusion.own = f32[4,8,8,8,128]{4,3,2,1,0:T(8,128)} fusion(f32[1,8,8,8,128]{4,3,2,1,0:T(8,128)S(1)} %broadcast_in_dim.2, f32[3,8,8,8,128]{4,3,2,1,0:T(8,128)S(1)} %bitcast.19), kind=kLoop, calls=%fused_computation | loop fusion | flops 262144 | bytes 2097152 | tf_op jit(solution)/shard_map/concatenate | solution.py:515
  4.2 4.6 %fusion = (f32[32,3,8,1,128]{4,3,2,1,0:T(1,128)}, f32[32,3,8,1,128]{4,3,2,1,0:T(1,128)}) fusion(f32[32,3,8,8,128]{4,3,2,1,0:T(8,128)} %res.1), kind=kLoop, calls=%fused_computation.4 | loop fusion | bytes 1572864 | tf_op jit(solution)/shard_map/slice | solution.py:333
  8.8 46.1 %shard_map.59 = (f32[256,32]{1,0:T(8,128)}, f32[72,32]{1,0:T(8,128)}, f32[2,32,3,8,128]{4,3,2,1,0:T(8,128)}, f32[2,32,3,8,128]{4,3,2,1,0:T(8,128)}, f32[4,12,12,8,128]{4,3,2,1,0:T(8,128)}) custom-call(f32[4,8,8,8,128]{4,3,2,1,0:T(8,128)} %pad_maximum_fusion.own, f32[6144,128]{1,0:T(8,128)} %bitcast.17, f32[32,3,8,8,128]{4,3,2,1,0:T(8,128)} %res.1, ...), custom_call_target="tpu_custom_call" | custom-call | tf_op jit(solution)/shard_map/pallas_call | solution.py:308
  54.9 1.3 %slice.11 = f32[8,32]{1,0:T(8,128)} slice(f32[72,32]{1,0:T(8,128)} %get-tuple-element.6), slice={[32:40], [0:32]} | slice | bytes 2048 | tf_op jit(solution)/shard_map/slice | solution.py:517
  56.2 0.8 copy.13
  57.0 0.0 copy-start
  57.0 1.7 %copy-done = f32[4,12,12,8,128]{4,3,2,1,0:T(8,128)S(1)} copy-done((f32[4,12,12,8,128]{4,3,2,1,0:T(8,128)S(1)}, f32[4,12,12,8,128]{4,3,2,1,0:T(8,128)}, u32[]{:S(2)}) %copy-start) | copy-done | bytes 2359320
  58.7 0.0 copy-start.1
  58.7 1.1 %copy-done.1 = f32[2,32,3,8,128]{4,3,2,1,0:T(8,128)S(1)} copy-done((f32[2,32,3,8,128]{4,3,2,1,0:T(8,128)S(1)}, f32[2,32,3,8,128]{4,3,2,1,0:T(8,128)}, u32[]{:S(2)}) %copy-start.1) | copy-done | bytes 786456
  59.8 0.0 copy-start.2
  59.9 1.1 %copy-done.2 = f32[2,32,3,8,128]{4,3,2,1,0:T(8,128)S(1)} copy-done((f32[2,32,3,8,128]{4,3,2,1,0:T(8,128)S(1)}, f32[2,32,3,8,128]{4,3,2,1,0:T(8,128)}, u32[]{:S(2)}) %copy-start.2) | copy-done | bytes 786456
  61.0 44.7 %shard_map.60 = f32[6144,128]{1,0:T(8,128)} custom-call(f32[6144,128]{1,0:T(8,128)} %bitcast.18, f32[4,12,12,8,128]{4,3,2,1,0:T(8,128)S(1)} %copy-done, f32[32,72]{1,0:T(8,128)S(1)} %bitcast.16, f32[1536,128]{1,0:T(8,128)S(1)} %bitcast.14, f32[1536,128]{1,0:T(8,128)S(1)} %bitcast.15), custom_call_target="tpu_custom_call" | custom-call | tf_op jit(solution)/shard_map/pallas_call | solution.py:484
  (1 shorter events, 0.0 us)
Async XLA Ops:
  57.0 1.7 %copy-start = (f32[4,12,12,8,128]{4,3,2,1,0:T(8,128)S(1)}, f32[4,12,12,8,128]{4,3,2,1,0:T(8,128)}, u32[]{:S(2)}) copy-start(f32[4,12,12,8,128]{4,3,2,1,0:T(8,128)} %get-tuple-element.7.ext) | copy-start | bytes 7077892
  58.7 1.1 %copy-start.1 = (f32[2,32,3,8,128]{4,3,2,1,0:T(8,128)S(1)}, f32[2,32,3,8,128]{4,3,2,1,0:T(8,128)}, u32[]{:S(2)}) copy-start(f32[2,32,3,8,128]{4,3,2,1,0:T(8,128)} %get-tuple-element.8) | copy-start | bytes 2359300
  59.8 1.1 %copy-start.2 = (f32[2,32,3,8,128]{4,3,2,1,0:T(8,128)S(1)}, f32[2,32,3,8,128]{4,3,2,1,0:T(8,128)}, u32[]{:S(2)}) copy-start(f32[2,32,3,8,128]{4,3,2,1,0:T(8,128)} %get-tuple-element.9) | copy-start | bytes 2359300

commit v2 on v1

--- a/solution.py
+++ b/solution.py
@@ -94,9 +94,9 @@
 
 
 def coarse_kernel(
-    count_x, count_y, width, own, flat, res, south_face, north_face,
+    count_x, count_y, width, own, flat, res,
     coeffs, grid, halo_x, halo_y, ext,
-    panel, gathered, send_sem, recv_sem, halo_send, halo_recv
+    panel, gathered, faces, send_sem, recv_sem, halo_send, halo_recv
 ):
     index_x = lax.axis_index("gx")
     index_y = lax.axis_index("yz")
@@ -133,6 +133,15 @@
         return carry
 
     lax.fori_loop(1, count, greet, 0)
+
+    def cut(r, carry):
+        for f in range(parts):
+            base = pl.multiple_of((r * parts + f) * depth * breadth, breadth)
+            for side in range(2):
+                faces[side, r, f] = flat[pl.ds(base + side * (breadth - 1), depth, stride=breadth), :]
+        return carry
+
+    lax.fori_loop(0, rhs, cut, 0)
     pl.semaphore_wait(barrier, count - 1)
 
     def can(dx, dy):
@@ -170,14 +179,18 @@
     cells = depth * breadth
 
     def loads(i, sums):
-        f = i // cells
-        cell = i - f * cells
-        v = own[f, cell // breadth, lax.rem(cell, breadth)]
-        return tuple(
-            total + v * flat[pl.ds(r * parts * cells + i, 1), :] for r, total in enumerate(sums)
-        )
-
-    sums = lax.fori_loop(0, parts * cells, loads, (zero,) * rhs)
+        f = i // depth
+        x = i - f * depth
+        base = pl.multiple_of(i * breadth, breadth)
+        for y in range(breadth):
+            v = own[f, x, y]
+            sums = tuple(
+                total + v * flat[pl.ds(base + r * parts * cells + y, 1), :]
+                for r, total in enumerate(sums)
+            )
+        return sums
+
+    sums = lax.fori_loop(0, parts * depth, loads, (zero,) * rhs)
     lane = lax.broadcasted_iota(jnp.int32, panel.shape, 1)
 
     def placed(total, at):
@@ -266,8 +279,8 @@
             start(own.at[:, x, y], ext.at[:, to_x, to_y], dx, dy)
     start(res.at[:, :, 0], halo_x.at[1], -1, 0)
     start(res.at[:, :, depth - 1], halo_x.at[0], 1, 0)
-    start(south_face, halo_y.at[1], 0, -1)
-    start(north_face, halo_y.at[0], 0, 1)
+    start(faces.at[0], halo_y.at[1], 0, -1)
+    start(faces.at[1], halo_y.at[0], 0, 1)
 
     def collect(step, carry):
         other = lax.rem(me + step, count)
@@ -278,13 +291,14 @@
     rows = [gathered[pl.ds(g * count_y, count_y)].reshape(size, length) for g in range(count_x)]
     for g, x in enumerate(cyclic_solve(rows, size)):
         coeffs[pl.ds(g * size, size), :] = x
+    grid[...] = jnp.zeros(grid.shape, jnp.float32)
     slot = 0
     for step_x in (-1, 0, 1):
         for step_y in (-1, 0, 1):
             near_x = jnp.clip(index_x + step_x, 0, count_x - 1)
             near_y = jnp.clip(index_y + step_y, 0, count_y - 1)
             begin = pl.multiple_of((near_x * count_y + near_y) * width, width)
-            grid[pl.ds(slot * width, width), :] = coeffs[pl.ds(begin, width), :]
+            grid[pl.ds(slot * width, width), pl.ds(0, rhs)] = coeffs[pl.ds(begin, width), :]
             slot += 1
 
     def drain(step, carry):
@@ -309,16 +323,17 @@
         functools.partial(coarse_kernel, count_x, count_y, width),
         out_shape=(
             jax.ShapeDtypeStruct((count * width, rhs), jnp.float32),
-            jax.ShapeDtypeStruct((9 * width, rhs), jnp.float32),
+            jax.ShapeDtypeStruct((pl.cdiv(9 * width, 128) * 128, pl.cdiv(rhs, 128) * 128), jnp.float32),
             jax.ShapeDtypeStruct((2, rhs, parts, breadth, length), jnp.float32),
             jax.ShapeDtypeStruct((2, rhs, parts, depth, length), jnp.float32),
             jax.ShapeDtypeStruct((fields, depth + 4, breadth + 4, width, length), jnp.float32),
         ),
-        in_specs=[vmem, vmem, hbm, hbm, hbm],
+        in_specs=[vmem, vmem, hbm],
         out_specs=(vmem, vmem, hbm, hbm, vmem),
         scratch_shapes=[
             pltpu.VMEM(panel, jnp.float32),
             pltpu.VMEM((count,) + panel, jnp.float32),
+            pltpu.VMEM((2, rhs, parts, depth, length), jnp.float32),
             pltpu.SemaphoreType.DMA((count,)),
             pltpu.SemaphoreType.DMA((count,)),
             pltpu.SemaphoreType.DMA((16,)),
@@ -329,68 +344,88 @@
         own,
         residuals.reshape(-1, length),
         residuals,
-        residuals[:, :, :, 0, :],
-        residuals[:, :, :, -1, :],
     )
 
 
 def schwarz_kernel(
-    rhs, parts, depth, breadth, width, res, ext, cgrid, halo_x, halo_y, out,
+    rhs, parts, depth, breadth, width, res, ext, cgrid, halo_x, halo_y, out, mine,
     weights, coeff, corr, forced, first, second
 ):
     length = res.shape[1]
     wide = breadth + 4
     own = depth * breadth
 
-    for cls in range(9):
-        for k in range(width):
-            coeff[cls * width + k] = jnp.broadcast_to(
-                cgrid[:, cls * width + k : cls * width + k + 1], (rhs, length)
-            )
+    mine[...] = cgrid[pl.ds(4 * width, width), pl.ds(0, rhs)]
+    turned = cgrid[...].T
+    for i in range(9 * width):
+        coeff[i] = jnp.broadcast_to(turned[:rhs, i : i + 1], (rhs, length))
     zero = jnp.zeros((rhs, length), jnp.float32)
-    for buffer in (first, second):
-        def clear(i, carry, buffer=buffer):
-            buffer[i] = zero
+    for buffer in (forced, first, second):
+        def clear_x(y, carry, buffer=buffer):
+            buffer[y] = zero
+            buffer[(depth + 3) * wide + y] = zero
             return carry
 
-        lax.fori_loop(0, (depth + 4) * wide, clear, 0)
+        def clear_y(x, carry, buffer=buffer):
+            buffer[x * wide] = zero
+            buffer[x * wide + wide - 1] = zero
+            return carry
+
+        lax.fori_loop(0, wide, clear_x, 0)
+        lax.fori_loop(0, depth + 4, clear_y, 0)
+        for x in (1, depth + 2):
+            for y in (1, breadth + 2):
+                buffer[x * wide + y] = zero
 
     def weigh(i, carry):
-        x = i // (breadth + 2) + 1
-        y = lax.rem(i, breadth + 2) + 1
-        m, diagonal, faces = cell_weights(ext, x, y)
-        scale = jnp.where(m > 0, 0.8, 0.0) / diagonal
-        weights[i, 0] = scale
-        for q, w in enumerate(faces):
-            weights[i, q + 1] = scale * w
-        return carry
-
-    lax.fori_loop(0, (depth + 2) * (breadth + 2), weigh, 0)
+        for y in range(breadth + 2):
+            m, diagonal, faces = cell_weights(ext, i + 1, y + 1)
+            scale = jnp.where(m > 0, 0.8, 0.0) / diagonal
+            at = i * (breadth + 2) + y
+            weights[at, 0] = scale
+            for q, w in enumerate(faces):
+                weights[at, q + 1] = scale * w
+        return carry
+
+    lax.fori_loop(0, depth + 2, weigh, 0)
 
     def spread(w, q):
         return jnp.concatenate([weights[w, q]] * (rhs // width), axis=0)
 
     def component(part, carry):
-        def region(cls, x0, nx, y0, ny):
+        def correct(cls, cells):
+            values = [None] * len(cells)
+            for k in range(width):
+                c = coeff[cls * width + k]
+                for i, (x, y) in enumerate(cells):
+                    term = c * ext[part, x, y, pl.ds(k, 1), :]
+                    values[i] = term if k == 0 else values[i] + term
+            for (x, y), value in zip(cells, values):
+                corr[x * wide + y] = value
+
+        def along_y(cls, x0, nx):
             def one(i, carry):
-                x = x0 + i // ny
-                y = y0 + lax.rem(i, ny)
-                value = coeff[cls * width] * ext[part, x, y, pl.ds(0, 1), :]
-                for k in range(1, width):
-                    value = value + coeff[cls * width + k] * ext[part, x, y, pl.ds(k, 1), :]
-                corr[x * wide + y] = value
+                correct(cls, [(x0 + i, y + 2) for y in range(breadth)])
                 return carry
 
-            lax.fori_loop(0, nx * ny, one, 0, unroll=2 if nx * ny > 1 else 1)
-
-        spans_x = ((0, 2), (2, depth), (depth + 2, 2))
-        spans_y = ((0, 2), (2, breadth), (breadth + 2, 2))
-        for a, (x0, nx) in enumerate(spans_x):
-            for b, (y0, ny) in enumerate(spans_y):
-                if a != 1 and b != 1:
-                    region(a * 3 + b, 1 if a == 0 else x0, 1, 1 if b == 0 else y0, 1)
-                else:
-                    region(a * 3 + b, x0, nx, y0, ny)
+            lax.fori_loop(0, nx, one, 0)
+
+        def along_x(cls, y0):
+            def one(i, carry):
+                correct(cls, [(x + 2, y0 + i) for x in range(depth)])
+                return carry
+
+            lax.fori_loop(0, 2, one, 0)
+
+        along_y(4, 2, depth)
+        along_y(1, 0, 2)
+        along_y(7, depth + 2, 2)
+        along_x(3, 0)
+        along_x(5, breadth + 2)
+        for cls, x, y in (
+            (0, 1, 1), (2, 1, breadth + 2), (6, depth + 2, 1), (8, depth + 2, breadth + 2)
+        ):
+            correct(cls, [(x, y)])
 
         def beside(buffer, x, y):
             cell = x * wide + y
@@ -412,9 +447,7 @@
             term = scale * loaded
             if outer:
                 term = jnp.where(scale > 0, term, 0.0)
-            value = term - 0.8 * centre + total
-            forced[cell] = value
-            first[cell] = value
+            forced[cell] = term - 0.8 * centre + total
 
         def force_row(i, carry):
             for y in range(breadth):
@@ -437,19 +470,21 @@
 
         lax.fori_loop(0, breadth, force_edge, 0)
 
-        source, target = first, second
+        source, target, spare = forced, first, second
         for sweep in range(1, SWEEPS):
             last = sweep == SWEEPS - 1
 
-            def relax(x, y, source=source, target=target):
+            def relaxed(x, y, source=source, opening=sweep == 1):
                 centre, total = beside(source, x, y)
-                cell = x * wide + y
-                target[cell] = 0.2 * centre + (forced[cell] + total)
-
-            def finish(x, y, source=source):
-                centre, total = beside(source, x, y)
-                cell = x * wide + y
-                value = corr[cell] + (0.2 * centre + (forced[cell] + total))
+                if opening:
+                    return 1.2 * centre + total
+                return 0.2 * centre + (forced[x * wide + y] + total)
+
+            def relax(x, y, target=target, relaxed=relaxed):
+                target[x * wide + y] = relaxed(x, y)
+
+            def finish(x, y, relaxed=relaxed):
+                value = corr[x * wide + y] + relaxed(x, y)
                 start = part * own + (x - 2) * breadth + y - 2
                 out[pl.ds(start, rhs, stride=parts * own), :] = value
 
@@ -470,7 +505,7 @@
                     return carry
 
                 lax.fori_loop(0, breadth, edge, 0)
-            source, target = target, source
+            source, target, spare = target, spare, target
         return carry
 
     lax.fori_loop(0, parts, component, 0)
@@ -481,11 +516,14 @@
     width = ext.shape[3]
     vmem = pl.BlockSpec(memory_space=pltpu.VMEM)
     field = pltpu.VMEM(((depth + 4) * (breadth + 4), rhs, length), jnp.float32)
-    result = pl.pallas_call(
+    result, coeffs = pl.pallas_call(
         functools.partial(schwarz_kernel, rhs, parts, depth, breadth, width),
-        out_shape=jax.ShapeDtypeStruct((rhs * parts * depth * breadth, length), jnp.float32),
+        out_shape=(
+            jax.ShapeDtypeStruct((rhs * parts * depth * breadth, length), jnp.float32),
+            jax.ShapeDtypeStruct((width, rhs), jnp.float32),
+        ),
         in_specs=[vmem] * 5,
-        out_specs=vmem,
+        out_specs=(vmem, vmem),
         scratch_shapes=[
             pltpu.VMEM(((depth + 2) * (breadth + 2), 7, width, length), jnp.float32),
             pltpu.VMEM((9 * width, rhs, length), jnp.float32),
@@ -495,11 +533,11 @@
     )(
         residuals.reshape(-1, length),
         ext,
-        grid.T,
+        grid,
         halo_x.reshape(-1, length),
         halo_y.reshape(-1, length),
     )
-    return result.reshape(residuals.shape)
+    return coeffs, result.reshape(residuals.shape)
 
 
 def on_device(residuals, vectors, phases, stiffness):
@@ -513,10 +551,8 @@
     modulus = jnp.sum(stiffness[:, None, None, None] * choose, axis=0)
     spread = jnp.broadcast_to(modulus[None, :, :, None, :], (1,) + modulus.shape[:2] + (width, modulus.shape[2]))
     own = jnp.concatenate([vectors.transpose(1, 2, 3, 0, 4), spread], axis=0)
-    coeffs_all, grid, halo_x, halo_y, ext = coarse_solve(own, residuals, count_x, count_y)
-    coeffs = grid[4 * width : 5 * width]
-    result = schwarz(residuals, ext, grid, halo_x, halo_y)
-    return (coeffs, result)
+    _, grid, halo_x, halo_y, ext = coarse_solve(own, residuals, count_x, count_y)
+    return schwarz(residuals, ext, grid, halo_x, halo_y)
 
 
 def solution(mesh):

time: 106 us -> 89 us (0.84)
  Pallas kernels: 90.9 us -> 79.5 us
  local copies, waits for them, and re-layouts: 12.2 us -> 6.38 us
    pallas_call x1, Pallas kernels: 44.7 us -> 33.6 us  [schwarz(): pl.pallas_call(functools.partial(schwarz_kernel, rhs, parts, depth, bread...]
    slice x2 -> x0, local copies, waits for them, and re-layouts: 5.84 us -> none  [the longest x1 4.57 us: coarse_solve(): residuals[:, :, :, -1, :]]
    unnamed x7 -> x9, local copies, waits for them, and re-layouts: 5.54 us -> 6.36 us
where the time goes in v2:
time: 89 us; the launch traced here: 88.5 us
  Pallas kernels  79.5 us (89%)
  local copies, waits for them, and re-layouts  6.38 us (7%)
  other arithmetic  1.95 us (2%)
    pallas_call x1, Pallas kernels, coarse_solve(): pl.pallas_call(functools.partial(coarse_kernel, count_x, count_y, width),...  45.9 us
    pallas_call x1, Pallas kernels, schwarz(): pl.pallas_call(functools.partial(schwarz_kernel, rhs, parts, depth, bread...  33.6 us
    unnamed x9, local copies, waits for them, and re-layouts  6.36 us

profile of v2, /device:TPU:9, one launch (start us, length us, event | category | flops | bytes accessed | tf_op | source)
XLA Modules:
  0.0 88.5 jit_solution(15522630902242222469)
XLA Ops:
  0.6 0.9 select_reduce_fusion
  1.5 1.6 %copy.9 = f32[8,3,8,8,128]{4,0,3,2,1:T(8,128)S(1)} copy(f32[8,3,8,8,128]{4,3,2,1,0:T(8,128)} %param.5) | data formatting | bytes 1572864 | tf_op args[1]
  3.1 1.1 %pad_maximum_fusion.own = f32[4,8,8,8,128]{4,3,2,1,0:T(8,128)} fusion(f32[1,8,8,8,128]{4,3,2,1,0:T(8,128)S(1)} %broadcast_in_dim.2, f32[3,8,8,8,128]{4,3,2,1,0:T(8,128)S(1)} %bitcast.11), kind=kLoop, calls=%fused_computation | loop fusion | flops 262144 | bytes 2097152 | tf_op jit(solution)/shard_map/concatenate | solution.py:553
  4.2 45.9 %shard_map.59 = (f32[256,32]{1,0:T(8,128)}, f32[128,128]{1,0:T(8,128)}, f32[2,32,3,8,128]{4,3,2,1,0:T(8,128)}, f32[2,32,3,8,128]{4,3,2,1,0:T(8,128)}, f32[4,12,12,8,128]{4,3,2,1,0:T(8,128)}) custom-call(f32[4,8,8,8,128]{4,3,2,1,0:T(8,128)} %pad_maximum_fusion.own, f32[6144,128]{1,0:T(8,128)} %bitcast.9, f32[32,3,8,8,128]{4,3,2,1,0:T(8,128)} %res.1), custom_call_target="tpu_custom_call" | custom-call | tf_op jit(solution)/shard_map/pallas_call | solution.py:322
  50.1 0.0 copy-start
  50.1 1.7 %copy-done = f32[4,12,12,8,128]{4,3,2,1,0:T(8,128)S(1)} copy-done((f32[4,12,12,8,128]{4,3,2,1,0:T(8,128)S(1)}, f32[4,12,12,8,128]{4,3,2,1,0:T(8,128)}, u32[]{:S(2)}) %copy-start) | copy-done | bytes 2359320
  51.7 0.0 copy-start.1
  51.8 1.1 %copy-done.1 = f32[2,32,3,8,128]{4,3,2,1,0:T(8,128)S(1)} copy-done((f32[2,32,3,8,128]{4,3,2,1,0:T(8,128)S(1)}, f32[2,32,3,8,128]{4,3,2,1,0:T(8,128)}, u32[]{:S(2)}) %copy-start.1) | copy-done | bytes 786456
  52.9 0.0 copy-start.2
  52.9 1.1 %copy-done.2 = f32[2,32,3,8,128]{4,3,2,1,0:T(8,128)S(1)} copy-done((f32[2,32,3,8,128]{4,3,2,1,0:T(8,128)S(1)}, f32[2,32,3,8,128]{4,3,2,1,0:T(8,128)}, u32[]{:S(2)}) %copy-start.2) | copy-done | bytes 786456
  54.0 0.0 copy-start.3
  54.0 0.8 copy-done.3
  54.9 33.6 %shard_map.60 = (f32[6144,128]{1,0:T(8,128)}, f32[8,32]{1,0:T(8,128)}) custom-call(f32[6144,128]{1,0:T(8,128)} %bitcast.10, f32[4,12,12,8,128]{4,3,2,1,0:T(8,128)S(1)} %copy-done, f32[128,128]{1,0:T(8,128)S(1)} %copy-done.3, f32[1536,128]{1,0:T(8,128)S(1)} %bitcast.7, f32[1536,128]{1,0:T(8,128)S(1)} %bitcast.8), custom_call_target="tpu_custom_call" | custom-call | tf_op jit(solution)/shard_map/pallas_call | solution.py:519
  (1 shorter events, 0.0 us)
Async XLA Ops:
  50.1 1.7 %copy-start = (f32[4,12,12,8,128]{4,3,2,1,0:T(8,128)S(1)}, f32[4,12,12,8,128]{4,3,2,1,0:T(8,128)}, u32[]{:S(2)}) copy-start(f32[4,12,12,8,128]{4,3,2,1,0:T(8,128)} %get-tuple-element.8.ext) | copy-start | bytes 7077892
  51.7 1.1 %copy-start.1 = (f32[2,32,3,8,128]{4,3,2,1,0:T(8,128)S(1)}, f32[2,32,3,8,128]{4,3,2,1,0:T(8,128)}, u32[]{:S(2)}) copy-start(f32[2,32,3,8,128]{4,3,2,1,0:T(8,128)} %get-tuple-element.10) | copy-start | bytes 2359300
  52.9 1.1 %copy-start.2 = (f32[2,32,3,8,128]{4,3,2,1,0:T(8,128)S(1)}, f32[2,32,3,8,128]{4,3,2,1,0:T(8,128)}, u32[]{:S(2)}) copy-start(f32[2,32,3,8,128]{4,3,2,1,0:T(8,128)} %get-tuple-element.11) | copy-start | bytes 2359300
  54.0 0.8 copy-start.3

commit v3 on v2

--- a/solution.py
+++ b/solution.py
@@ -117,14 +117,6 @@
 
     lax.fori_loop(0, depth + 4, clear, 0)
 
-    def fill(x, carry):
-        for f in range(fields):
-            for y in range(breadth):
-                ext[f, x + 2, y + 2] = own[f, x, y]
-        return carry
-
-    lax.fori_loop(0, depth, fill, 0)
-
     def greet(step, carry):
         other = lax.rem(me + step, count)
         pl.semaphore_signal(
@@ -175,7 +167,23 @@
         start(own.at[:, :, step], ext.at[:, inner_x, breadth + 2 + step], 0, -1)
         start(own.at[:, :, breadth - 1 - step], ext.at[:, inner_x, 1 - step], 0, 1)
 
+    def rows(low, count):
+        part = pl.ds(low, count)
+        start(res.at[part, :, 0], halo_x.at[1, part], -1, 0)
+        start(res.at[part, :, depth - 1], halo_x.at[0, part], 1, 0)
+
+    early = rhs * 3 // 8
     layer(0)
+    first = len(started)
+    rows(0, early)
+    def fill(x, carry):
+        for f in range(fields):
+            for y in range(breadth):
+                ext[f, x + 2, y + 2] = own[f, x, y]
+        return carry
+
+    lax.fori_loop(0, depth, fill, 0)
+
     cells = depth * breadth
 
     def loads(i, sums):
@@ -200,7 +208,7 @@
     row = jnp.zeros(panel.shape, jnp.float32)
     for r in range(rhs):
         row = row + placed(sums[r], 3 * size + r)
-    for _, receives, copy in started:
+    for _, receives, copy in started[:first]:
         pl.when(receives)(copy.wait_recv)
 
     def gram(sums, left, f, x, y):
@@ -270,15 +278,13 @@
         return carry
 
     lax.fori_loop(1, count, send, 0)
-    first = len(started)
+    rows(early, rhs - early)
     layer(1)
     ends_x = ((0, -1, depth + 2), (depth - 1, 1, 1))
     ends_y = ((0, -1, breadth + 2), (breadth - 1, 1, 1))
     for x, dx, to_x in ends_x:
         for y, dy, to_y in ends_y:
             start(own.at[:, x, y], ext.at[:, to_x, to_y], dx, dy)
-    start(res.at[:, :, 0], halo_x.at[1], -1, 0)
-    start(res.at[:, :, depth - 1], halo_x.at[0], 1, 0)
     start(faces.at[0], halo_y.at[1], 0, -1)
     start(faces.at[1], halo_y.at[0], 0, 1)
 
@@ -288,8 +294,8 @@
         return carry
 
     lax.fori_loop(1, count, collect, 0)
-    rows = [gathered[pl.ds(g * count_y, count_y)].reshape(size, length) for g in range(count_x)]
-    for g, x in enumerate(cyclic_solve(rows, size)):
+    panels = [gathered[pl.ds(g * count_y, count_y)].reshape(size, length) for g in range(count_x)]
+    for g, x in enumerate(cyclic_solve(panels, size)):
         coeffs[pl.ds(g * size, size), :] = x
     grid[...] = jnp.zeros(grid.shape, jnp.float32)
     slot = 0
@@ -336,8 +342,8 @@
             pltpu.VMEM((2, rhs, parts, depth, length), jnp.float32),
             pltpu.SemaphoreType.DMA((count,)),
             pltpu.SemaphoreType.DMA((count,)),
-            pltpu.SemaphoreType.DMA((16,)),
-            pltpu.SemaphoreType.DMA((16,)),
+            pltpu.SemaphoreType.DMA((18,)),
+            pltpu.SemaphoreType.DMA((18,)),
         ],
         compiler_params=pltpu.CompilerParams(collective_id=0, has_side_effects=True),
     )(
@@ -348,11 +354,24 @@
 
 
 def schwarz_kernel(
-    rhs, parts, depth, breadth, width, res, ext, cgrid, halo_x, halo_y, out, mine,
+    rhs, parts, depth, breadth, width, res_any, ext_any, cgrid, halo_x_any, halo_y_any, out_any, mine,
+    res, ext, halo_x, halo_y, out, load_sem, ext_sem, out_sem,
     weights, coeff, corr, forced, first, second
 ):
     length = res.shape[1]
     wide = breadth + 4
+
+    def load_field(f):
+        return pltpu.make_async_copy(ext_any.at[f], ext.at[f], ext_sem.at[f])
+
+    loads = [
+        pltpu.make_async_copy(source, target, load_sem.at[i])
+        for i, (source, target) in enumerate(((res_any, res), (halo_x_any, halo_x), (halo_y_any, halo_y)))
+    ]
+    for f in (parts, *range(parts)):
+        load_field(f).start()
+    for copy in loads:
+        copy.start()
     own = depth * breadth
 
     mine[...] = cgrid[pl.ds(4 * width, width), pl.ds(0, rhs)]
@@ -377,6 +396,8 @@
             for y in (1, breadth + 2):
                 buffer[x * wide + y] = zero
 
+    load_field(parts).wait()
+
     def weigh(i, carry):
         for y in range(breadth + 2):
             m, diagonal, faces = cell_weights(ext, i + 1, y + 1)
@@ -393,6 +414,8 @@
         return jnp.concatenate([weights[w, q]] * (rhs // width), axis=0)
 
     def component(part, carry):
+        load_field(part).wait()
+
         def correct(cls, cells):
             values = [None] * len(cells)
             for k in range(width):
@@ -459,6 +482,11 @@
                 force(i + 2, 1 + side * (breadth + 1), loaded, True)
             return carry
 
+        @pl.when(part == 0)
+        def _():
+            for copy in loads:
+                copy.wait()
+
         lax.fori_loop(0, depth, force_row, 0)
 
         def force_edge(i, carry):
@@ -485,8 +513,8 @@
 
             def finish(x, y, relaxed=relaxed):
                 value = corr[x * wide + y] + relaxed(x, y)
-                start = part * own + (x - 2) * breadth + y - 2
-                out[pl.ds(start, rhs, stride=parts * own), :] = value
+                start = part * rhs * own + (x - 2) * breadth + y - 2
+                out[pl.ds(start, rhs, stride=own), :] = value
 
             def row(i, carry, last=last, relax=relax, finish=finish):
                 if last:
@@ -506,15 +534,27 @@
 
                 lax.fori_loop(0, breadth, edge, 0)
             source, target, spare = target, spare, target
+
+        def write(r, carry):
+            pltpu.make_async_copy(
+                out.at[pl.ds(pl.multiple_of((part * rhs + r) * own, own), own)],
+                out_any.at[pl.ds(pl.multiple_of((r * parts + part) * own, own), own)],
+                out_sem,
+            ).start()
+            return carry
+
+        lax.fori_loop(0, rhs, write, 0)
         return carry
 
     lax.fori_loop(0, parts, component, 0)
+    pltpu.make_async_copy(out, out_any, out_sem).wait()
 
 
 def schwarz(residuals, ext, grid, halo_x, halo_y):
     rhs, parts, depth, breadth, length = residuals.shape
     width = ext.shape[3]
     vmem = pl.BlockSpec(memory_space=pltpu.VMEM)
+    hbm = pl.BlockSpec(memory_space=pl.ANY)
     field = pltpu.VMEM(((depth + 4) * (breadth + 4), rhs, length), jnp.float32)
     result, coeffs = pl.pallas_call(
         functools.partial(schwarz_kernel, rhs, parts, depth, breadth, width),
@@ -522,14 +562,22 @@
             jax.ShapeDtypeStruct((rhs * parts * depth * breadth, length), jnp.float32),
             jax.ShapeDtypeStruct((width, rhs), jnp.float32),
         ),
-        in_specs=[vmem] * 5,
-        out_specs=(vmem, vmem),
+        in_specs=[hbm, hbm, vmem, hbm, hbm],
+        out_specs=(hbm, vmem),
         scratch_shapes=[
+            pltpu.VMEM((residuals.size // length, length), jnp.float32),
+            pltpu.VMEM(ext.shape, jnp.float32),
+            pltpu.VMEM((halo_x.size // length, length), jnp.float32),
+            pltpu.VMEM((halo_y.size // length, length), jnp.float32),
+            pltpu.VMEM((residuals.size // length, length), jnp.float32),
+            pltpu.SemaphoreType.DMA((3,)),
+            pltpu.SemaphoreType.DMA((parts + 1,)),
+            pltpu.SemaphoreType.DMA,
             pltpu.VMEM(((depth + 2) * (breadth + 2), 7, width, length), jnp.float32),
             pltpu.VMEM((9 * width, rhs, length), jnp.float32),
             field, field, field, field,
         ],
-        compiler_params=pltpu.CompilerParams(vmem_limit_bytes=48 * 1024 * 1024),
+        compiler_params=pltpu.CompilerParams(vmem_limit_bytes=63 * 1024 * 1024),
     )(
         residuals.reshape(-1, length),
         ext,

time: 89 us -> 80.5 us (0.904)
  local copies, waits for them, and re-layouts: 6.38 us -> 1.61 us
  Pallas kernels: 79.5 us -> 75.9 us
    unnamed x9 -> x1, local copies, waits for them, and re-layouts: 6.36 us -> 1.59 us
    pallas_call x1, Pallas kernels: 45.9 us -> 42.9 us  [coarse_solve(): pl.pallas_call(functools.partial(coarse_kernel, count_x, count_y, width),...]
where the time goes in v3:
time: 80.5 us; the launch traced here: 80.2 us
  Pallas kernels  75.9 us (94%)
  other arithmetic  1.95 us (2%)
  local copies, waits for them, and re-layouts  1.61 us (2%)
    pallas_call x1, Pallas kernels, coarse_solve(): pl.pallas_call(functools.partial(coarse_kernel, count_x, count_y, width),...  42.9 us
    pallas_call x1, Pallas kernels, schwarz(): pl.pallas_call(functools.partial(schwarz_kernel, rhs, parts, depth, bread...  33.1 us

profile of v3, /device:TPU:9, one launch (start us, length us, event | category | flops | bytes accessed | tf_op | source)
XLA Modules:
  0.0 80.2 jit_solution(5343908863425100768)
XLA Ops:
  0.6 0.9 %select_reduce_fusion = f32[8,8,128]{2,1,0:T(8,128)S(1)} fusion(f32[8]{0:T(128)} %param.7, s32[8,8,128]{2,1,0:T(8,128)} %param.6), kind=kLoop, calls=%fused_computation.2 | loop fusion | flops 188416 | bytes 65568 | tf_op jit(solution)/shard_map/reduce_sum | solution.py:599
  1.5 1.6 %copy.9 = f32[8,3,8,8,128]{4,0,3,2,1:T(8,128)S(1)} copy(f32[8,3,8,8,128]{4,3,2,1,0:T(8,128)} %param.5) | data formatting | bytes 1572864 | tf_op args[1]
  3.1 1.1 %pad_maximum_fusion.own = f32[4,8,8,8,128]{4,3,2,1,0:T(8,128)} fusion(f32[1,8,8,8,128]{4,3,2,1,0:T(8,128)S(1)} %broadcast_in_dim.2, f32[3,8,8,8,128]{4,3,2,1,0:T(8,128)S(1)} %bitcast.9), kind=kLoop, calls=%fused_computation | loop fusion | flops 262144 | bytes 2097152 | tf_op jit(solution)/shard_map/concatenate | solution.py:601
  4.2 42.9 %shard_map.59 = (f32[256,32]{1,0:T(8,128)}, f32[128,128]{1,0:T(8,128)}, f32[2,32,3,8,128]{4,3,2,1,0:T(8,128)}, f32[2,32,3,8,128]{4,3,2,1,0:T(8,128)}, f32[4,12,12,8,128]{4,3,2,1,0:T(8,128)}) custom-call(f32[4,8,8,8,128]{4,3,2,1,0:T(8,128)} %pad_maximum_fusion.own, f32[6144,128]{1,0:T(8,128)} %bitcast.7, f32[32,3,8,8,128]{4,3,2,1,0:T(8,128)} %res.1), custom_call_target="tpu_custom_call" | custom-call | tf_op jit(solution)/shard_map/pallas_call | solution.py:328
  47.1 33.1 %shard_map.60 = (f32[6144,128]{1,0:T(8,128)}, f32[8,32]{1,0:T(8,128)}) custom-call(f32[6144,128]{1,0:T(8,128)} %bitcast.8, f32[4,12,12,8,128]{4,3,2,1,0:T(8,128)} %get-tuple-element.8.ext_any, f32[128,128]{1,0:T(8,128)} %get-tuple-element.9.cgrid, f32[1536,128]{1,0:T(8,128)} %bitcast.10, f32[1536,128]{1,0:T(8,128)} %bitcast.11), custom_call_target="tpu_custom_call" | custom-call | tf_op jit(solution)/shard_map/pallas_call | solution.py:559
  (1 shorter events, 0.0 us)

commit v4 on v3

--- a/solution.py
+++ b/solution.py
@@ -176,6 +176,8 @@
     layer(0)
     first = len(started)
     rows(0, early)
+    start(faces.at[0], halo_y.at[1], 0, -1)
+    start(faces.at[1], halo_y.at[0], 0, 1)
     def fill(x, carry):
         for f in range(fields):
             for y in range(breadth):
@@ -285,8 +287,6 @@
     for x, dx, to_x in ends_x:
         for y, dy, to_y in ends_y:
             start(own.at[:, x, y], ext.at[:, to_x, to_y], dx, dy)
-    start(faces.at[0], halo_y.at[1], 0, -1)
-    start(faces.at[1], halo_y.at[0], 0, 1)
 
     def collect(step, carry):
         other = lax.rem(me + step, count)

time: 80.5 us -> 80.5 us (level)
  no operation moved by 1% of the time
where the time goes in v4:
time: 80.5 us; the launch traced here: 80.2 us
  Pallas kernels  75.9 us (94%)
  other arithmetic  1.95 us (2%)
  local copies, waits for them, and re-layouts  1.61 us (2%)
    pallas_call x1, Pallas kernels, coarse_solve(): pl.pallas_call(functools.partial(coarse_kernel, count_x, count_y, width),...  42.9 us
    pallas_call x1, Pallas kernels, schwarz(): pl.pallas_call(functools.partial(schwarz_kernel, rhs, parts, depth, bread...  33.1 us

profile of v4, /device:TPU:9, one launch (start us, length us, event | category | flops | bytes accessed | tf_op | source)
XLA Modules:
  0.0 80.2 jit_solution(12381360197691331878)
XLA Ops:
  0.6 0.9 %select_reduce_fusion = f32[8,8,128]{2,1,0:T(8,128)S(1)} fusion(f32[8]{0:T(128)} %param.7, s32[8,8,128]{2,1,0:T(8,128)} %param.6), kind=kLoop, calls=%fused_computation.2 | loop fusion | flops 188416 | bytes 65568 | tf_op jit(solution)/shard_map/reduce_sum | solution.py:599
  1.5 1.6 %copy.9 = f32[8,3,8,8,128]{4,0,3,2,1:T(8,128)S(1)} copy(f32[8,3,8,8,128]{4,3,2,1,0:T(8,128)} %param.5) | data formatting | bytes 1572864 | tf_op args[1]
  3.1 1.1 %pad_maximum_fusion.own = f32[4,8,8,8,128]{4,3,2,1,0:T(8,128)} fusion(f32[1,8,8,8,128]{4,3,2,1,0:T(8,128)S(1)} %broadcast_in_dim.2, f32[3,8,8,8,128]{4,3,2,1,0:T(8,128)S(1)} %bitcast.9), kind=kLoop, calls=%fused_computation | loop fusion | flops 262144 | bytes 2097152 | tf_op jit(solution)/shard_map/concatenate | solution.py:601
  4.2 42.9 %shard_map.59 = (f32[256,32]{1,0:T(8,128)}, f32[128,128]{1,0:T(8,128)}, f32[2,32,3,8,128]{4,3,2,1,0:T(8,128)}, f32[2,32,3,8,128]{4,3,2,1,0:T(8,128)}, f32[4,12,12,8,128]{4,3,2,1,0:T(8,128)}) custom-call(f32[4,8,8,8,128]{4,3,2,1,0:T(8,128)} %pad_maximum_fusion.own, f32[6144,128]{1,0:T(8,128)} %bitcast.7, f32[32,3,8,8,128]{4,3,2,1,0:T(8,128)} %res.1), custom_call_target="tpu_custom_call" | custom-call | tf_op jit(solution)/shard_map/pallas_call | solution.py:328
  47.1 33.1 %shard_map.60 = (f32[6144,128]{1,0:T(8,128)}, f32[8,32]{1,0:T(8,128)}) custom-call(f32[6144,128]{1,0:T(8,128)} %bitcast.8, f32[4,12,12,8,128]{4,3,2,1,0:T(8,128)} %get-tuple-element.8.ext_any, f32[128,128]{1,0:T(8,128)} %get-tuple-element.9.cgrid, f32[1536,128]{1,0:T(8,128)} %bitcast.10, f32[1536,128]{1,0:T(8,128)} %bitcast.11), custom_call_target="tpu_custom_call" | custom-call | tf_op jit(solution)/shard_map/pallas_call | solution.py:559
  (1 shorter events, 0.0 us)
